TPU v7x, 128 devices: a whole 4x4x4 slice. The times are simulated.
128 devices in a mesh: ctx: 32 (over y, z, core), tp: 4 (over x).
Axes of the slice: x: 4, y: 4, z: 4, core: 2. Of those that a mesh axis runs over, the one named last changes fastest.
Arguments:
- query: bfloat16 [16384, 6144], P('ctx', 'tp'), may hold values from -6 to 6
- key_in: bfloat16 [16384, 6144], P('ctx', 'tp'), may hold values from -6 to 6
- value_in: bfloat16 [16384, 6144], P('ctx', 'tp'), may hold values from -6 to 6
- dout: bfloat16 [16384, 6144], P('ctx', 'tp'), may hold values from -0.5 to 0.5
- summary_offset: int32 [4], replicated, may hold values from 0 to 31
Outputs:
- grad_query: bfloat16 [16384, 6144], P(('ctx', 'tp'))
- grad_key: bfloat16 [16384, 6144], P(('ctx', 'tp'))
- grad_value: bfloat16 [16384, 6144], P(('ctx', 'tp'))
Inputs may be any that keep to these rules, and one draw needn't show every extreme that they name: Summary block s is block s * 32 + summary_offset[s].
All inputs are finite; a program needn't handle non-finite values.
Results may differ from a plain program's by a relative error of at most 0.014.
Values may be sent and summed in bfloat16 or wider, within the bound.
No kernel may reach another device: no remote copies, remote signals or barrier semaphores. Data moves between devices by JAX's collectives and lax.ppermute only.
A program may use at most 128 MiB of HBM per device.

v0:
```python
import functools
import math

import jax
import jax.numpy as jnp
from jax import lax
from jax.experimental import pallas as pl
from jax.experimental.pallas import tpu as pltpu
from jax.sharding import PartitionSpec as P


HDIM = 128
BLOCK = 128
BAND = 8
STRIDE = 32
CHIP_BLOCKS = 8
HALO = (BAND - 1) * BLOCK
OWN = CHIP_BLOCKS * BLOCK
EXT = HALO + OWN
TILE = 256
NSUM = 4
SPAN = 9
ROWS = (SPAN + NSUM) * BLOCK
NEG = -1e30
SIZES = (3, 3)
CHIPS = 16
SIDE = 4
SCALE = HDIM**-0.5
LOG2E = math.log2(math.e)
BF16 = jnp.bfloat16
F32 = jnp.float32


def ring(step):
    return [(2 * c + k, 2 * ((c + step) % CHIPS) + k) for c in range(CHIPS) for k in range(2)]


def along_z(step):
    return [
        (2 * (y * SIDE + z) + k, 2 * (y * SIDE + (z + step) % SIDE) + k)
        for y in range(SIDE)
        for z in range(SIDE)
        for k in range(2)
    ]


def along_y(step):
    return [
        (2 * (y * SIDE + z) + k, 2 * ((y + step) % SIDE * SIDE + z) + k)
        for y in range(SIDE)
        for z in range(SIDE)
        for k in range(2)
    ]


SWAP = [(d, d ^ 1) for d in range(2 * CHIPS)]


def along_x(step):
    return [(x, (x + step) % SIDE) for x in range(SIDE)]


def params(**kw):
    return pltpu.CompilerParams(vmem_limit_bytes=56 * 1024 * 1024, **kw)


def cost(flops, nbytes):
    return pl.CostEstimate(flops=flops, bytes_accessed=nbytes, transcendentals=0)


def whole(shape):
    return pl.BlockSpec(shape, lambda *_: (0,) * len(shape))


def pack_kernel(sc, off, *refs):
    ins, (own, oth) = refs[:8], refs[8:]
    for n in range(4):
        own[n] = ins[2 * n][...]
        oth[n] = ins[2 * n + 1][...]


def pack(sc, off, arrays, base, heads, width):
    rows = arrays[0].shape[0]
    half = width // HDIM // 2
    chunk = 256
    cols = heads * HDIM
    specs, args = [], []
    for array in arrays:
        for other in (0, 1):
            specs.append(
                pl.BlockSpec(
                    (chunk, cols),
                    lambda i, sc, off, other=other: (
                        i,
                        jnp.abs(sc[1] - other) * (half // heads) + base // heads,
                    ),
                )
            )
            args.append(array)
    out = pl.BlockSpec((4, chunk, cols), lambda i, sc, off: (0, i, 0))
    shape = jax.ShapeDtypeStruct((4, rows, cols), BF16)
    return pl.pallas_call(
        pack_kernel,
        grid_spec=pltpu.PrefetchScalarGridSpec(
            num_scalar_prefetch=2,
            grid=(rows // chunk,),
            in_specs=specs,
            out_specs=[out, out],
        ),
        out_shape=[shape, shape],
        compiler_params=params(),
        cost_estimate=cost(0, 16 * rows * cols * 2),
        name="pack",
    )(sc, off, *args)


def halo_kernel(sc, off, own, recv, qd, kv):
    lo = OWN // 2

    def fill(first, second):
        @pl.when(pl.program_id(0) < 2)
        def _():
            qd[:, :lo] = first[...]
            qd[:, lo:] = second[:, : lo - BLOCK]

        @pl.when(pl.program_id(0) >= 2)
        def _():
            kv[:, : lo - BLOCK] = first[:, BLOCK:]
            kv[:, lo - BLOCK :] = second[...]

    pl.when(sc[1] == 0)(lambda: fill(own, recv))
    pl.when(sc[1] == 1)(lambda: fill(recv, own))


def halo_of(sc, off, own, recv):
    width = own.shape[2]
    spec = pl.BlockSpec((1, OWN // 2, width), lambda i, sc, off: (i, 0, 0))
    return pl.pallas_call(
        halo_kernel,
        grid_spec=pltpu.PrefetchScalarGridSpec(
            num_scalar_prefetch=2,
            grid=(4,),
            in_specs=[spec, spec],
            out_specs=[
                pl.BlockSpec((1, HALO, width), lambda i, sc, off: (jnp.minimum(i, 1), 0, 0)),
                pl.BlockSpec((1, HALO, width), lambda i, sc, off: (jnp.maximum(i - 2, 0), 0, 0)),
            ],
        ),
        out_shape=[jax.ShapeDtypeStruct((2, HALO, width), BF16)] * 2,
        compiler_params=params(),
        cost_estimate=cost(0, 16 * OWN * width * 2),
        name="halo",
    )(sc, off, own, recv)


def candidate_kernel(sc, off, key, value, own, oth):
    half = own.shape[2]
    for n, ref in enumerate((key, value)):
        own[n] = ref[:, pl.ds(pl.multiple_of(sc[1] * half, HDIM), half)]
        oth[n] = ref[:, pl.ds(pl.multiple_of((1 - sc[1]) * half, HDIM), half)]


def candidate(sc, off, key, value):
    width = key.shape[1]
    spec = pl.BlockSpec((BLOCK, width), lambda i, sc, off: (off[sc[2]] & 3, 0))
    shape = (2, BLOCK, width // 2)
    return pl.pallas_call(
        candidate_kernel,
        grid_spec=pltpu.PrefetchScalarGridSpec(
            num_scalar_prefetch=2, grid=(1,), in_specs=[spec] * 2, out_specs=[whole(shape)] * 2
        ),
        out_shape=[jax.ShapeDtypeStruct(shape, BF16)] * 2,
        compiler_params=params(),
        cost_estimate=cost(0, 8 * BLOCK * width),
        name="candidate",
    )(sc, off, key, value)


def pieces_kernel(sc, off, own, recv, *outs):
    piece = BLOCK // SIDE
    mine = ((off[sc[2]] & 7) >> 2) == sc[1]
    for step in range(SIDE):
        row = pl.multiple_of(((sc[3] + step) & 3) * piece, piece)

        def put(ref, out=outs[step], row=row):
            out[...] = ref[:, pl.ds(row, piece), :]

        pl.when(mine)(functools.partial(put, own))
        pl.when(jnp.logical_not(mine))(functools.partial(put, recv))


def pieces_of(sc, off, own, recv):
    shape = (2, BLOCK // SIDE, own.shape[2])
    return pl.pallas_call(
        pieces_kernel,
        grid_spec=pltpu.PrefetchScalarGridSpec(
            num_scalar_prefetch=2,
            grid=(1,),
            in_specs=[whole(own.shape)] * 2,
            out_specs=[whole(shape)] * SIDE,
        ),
        out_shape=[jax.ShapeDtypeStruct(shape, BF16)] * SIDE,
        compiler_params=params(),
        cost_estimate=cost(0, 8 * own.size),
        name="pieces",
    )(sc, off, own, recv)


def gather_kernel(sc, off, *refs):
    out = refs[SIDE]
    piece = BLOCK // SIDE
    for step in range(SIDE):
        row = pl.multiple_of(((sc[3] + SIDE - step) % SIDE) * piece, piece)
        out[:, pl.ds(row, piece), :] = refs[step][...]


def gather(sc, off, pieces):
    shape = pieces[0].shape
    full = (2, BLOCK, shape[2])
    return pl.pallas_call(
        gather_kernel,
        grid_spec=pltpu.PrefetchScalarGridSpec(
            num_scalar_prefetch=2, grid=(1,), in_specs=[whole(shape)] * SIDE, out_specs=whole(full)
        ),
        out_shape=jax.ShapeDtypeStruct(full, BF16),
        compiler_params=params(),
        cost_estimate=cost(0, 4 * BLOCK * shape[2] * 2),
        name="gather",
    )(sc, off, *pieces)


def fold(x, op):
    return op(x.reshape(x.shape[0] // 8, 8, x.shape[1]), axis=0)


def spread(x):
    return x.reshape(x.shape[0] // 8, 8, x.shape[1])


def dot_nt(a, b):
    return lax.dot_general(a, b, (((1,), (1,)), ((), ())), preferred_element_type=F32)


def dot_nn(a, b):
    return lax.dot_general(a, b, (((1,), (0,)), ((), ())), preferred_element_type=F32)


def load_own(buf, own, recv, core, n, start):
    half = OWN // 2
    buf[pl.ds(pl.multiple_of(start + core * half, BLOCK), half), :] = own[n]
    buf[pl.ds(pl.multiple_of(start + (1 - core) * half, BLOCK), half), :] = recv[n]


def attn_kernel(sc, off, own, recv, halo, s0, s1, s2, s3, dq, dkv, stat, ds_out, *scratch):
    kx, vx, qs, dos, kxt, xs, dps, dsb, pb = scratch
    core, chip, y = sc[1], sc[0], sc[2]
    load_own(qs, own, recv, core, 0, 0)
    load_own(dos, own, recv, core, 1, 0)
    for buf, n in ((kx, 0), (vx, 1)):
        buf[0:HALO, :] = halo[n]
        load_own(buf, own, recv, core, 2 + n, HALO)
        for s, part in enumerate((s0, s1, s2, s3)):
            buf[EXT + s * BLOCK : EXT + (s + 1) * BLOCK, :] = part[n]
    kxt[...] = kx[...].T
    row = lax.broadcasted_iota(jnp.int32, (BLOCK, TILE), 0)
    col = lax.broadcasted_iota(jnp.int32, (BLOCK, TILE), 1)
    first = lax.broadcasted_iota(jnp.int32, (1, TILE), 1) < BLOCK
    outside = jnp.where(chip == 0, NEG, 0.0)

    for t in range(OWN // TILE):
        base = t * TILE
        q_t = qs[base : base + TILE, :]
        do_t = dos[base : base + TILE, :]

        def start_of(j, base=base):
            return base + j * BLOCK if j < SPAN else EXT + (j - SPAN) * BLOCK

        m8 = jnp.full((8, TILE), NEG, F32)
        l8 = jnp.zeros((8, TILE), F32)
        d8 = jnp.zeros((8, TILE), F32)
        tops = []
        for j in range(SPAN + NSUM):
            span = slice(j * BLOCK, (j + 1) * BLOCK)
            at = slice(start_of(j), start_of(j) + BLOCK)
            x = dot_nt(kx[at, :], q_t) * (SCALE * LOG2E)
            if start_of(j) < HALO:
                x = x + outside
            if j == 0:
                x = jnp.where(first, x, NEG)
            if j == BAND - 1:
                x = jnp.where(row <= col, x, NEG)
            if j == BAND:
                x = jnp.where(row + BLOCK <= col, x, NEG)
            if j >= SPAN:
                slot = (y + NSUM - (j - SPAN)) & 3
                g = slot * STRIDE + off[slot]
                block = chip * CHIP_BLOCKS + 2 * t - (BAND - 1)
                b0 = jnp.where(g < block, 0.0, NEG)
                b1 = jnp.where(g < block + 1, 0.0, NEG)
                x = x + jnp.where(first, b0, b1)
            dp = dot_nt(vx[at, :], do_t)
            top = jnp.maximum(m8, fold(x, jnp.max))
            fade = jnp.exp2(m8 - top)
            p = jnp.exp2(spread(x) - top[None])
            l8 = l8 * fade + jnp.sum(p, axis=0)
            d8 = d8 * fade + jnp.sum(p * spread(dp), axis=0)
            xs[span, :] = p.reshape(BLOCK, TILE)
            dps[span, :] = dp
            m8 = top
            tops.append(top)
        m = jnp.max(m8, axis=0, keepdims=True)
        rest = jnp.exp2(m8 - m)
        total = jnp.sum(l8 * rest, axis=0, keepdims=True)
        inv = 1.0 / total
        delta = jnp.sum(d8 * rest, axis=0, keepdims=True) * inv
        stat[0, 0:1, base : base + TILE] = m + jnp.log2(total)
        stat[0, 1:2, base : base + TILE] = delta
        for j in range(SPAN + NSUM):
            span = slice(j * BLOCK, (j + 1) * BLOCK)
            factor = jnp.exp2(tops[j] - m) * inv
            p = (spread(xs[span, :]) * factor[None]).reshape(BLOCK, TILE)
            at = start_of(j)
            cols = slice(base, base + TILE)
            dsb[at : at + BLOCK, cols] = (p * (dps[span, :] - delta)).astype(BF16)
            if at >= HALO:
                pb[at - HALO : at - HALO + BLOCK, cols] = p.astype(BF16)
        cols = slice(base, base + TILE)
        dqt = dot_nn(kxt[:, base : base + SPAN * BLOCK], dsb[base : base + SPAN * BLOCK, cols])
        dqt = dqt + dot_nn(kxt[:, EXT:], dsb[EXT:, cols])
        dq[base : base + TILE, :] = (dqt * SCALE).T.astype(BF16)

    for t in range(OWN // TILE):
        keys = slice(t * TILE, (t + 1) * TILE)
        dkv[0, keys, :] = dot_nn(dsb[HALO + t * TILE : HALO + (t + 1) * TILE, t * TILE :], qs[t * TILE :, :])
        dkv[1, keys, :] = dot_nn(pb[keys, t * TILE :], dos[t * TILE :, :])
    for s in range(NSUM // 2):
        keys = slice(s * TILE, (s + 1) * TILE)
        ds_out[0, keys, :] = (
            dot_nn(dsb[EXT + s * TILE : EXT + (s + 1) * TILE, :], qs[...]) * SCALE
        ).astype(BF16)
        ds_out[1, keys, :] = dot_nn(pb[OWN + s * TILE : OWN + (s + 1) * TILE, :], dos[...]).astype(BF16)


def later_kernel(sc, off, own, recv, qd, stat, dkv, out, kx, vx, qs, dos, dsb, pb):
    core, chip = sc[1], sc[0]
    load_own(kx, own, recv, core, 0, 0)
    load_own(vx, own, recv, core, 1, 0)
    for buf, n in ((qs, 0), (dos, 1)):
        buf[0:HALO, :] = qd[n]
        buf[HALO:, :] = jnp.zeros((OWN - HALO, HDIM), BF16)
    first = lax.broadcasted_iota(jnp.int32, (1, TILE), 1) < BLOCK
    outside = jnp.where(chip == CHIPS - 1, NEG, 0.0)
    for t in range(OWN // TILE):
        cols = slice(t * TILE, (t + 1) * TILE)
        q_t = qs[cols, :]
        do_t = dos[cols, :]
        shift = outside - stat[0, 0:1, cols]
        delta = stat[0, 1:2, cols]
        for j in range(2 * t + 1, CHIP_BLOCKS):
            at = slice(j * BLOCK, (j + 1) * BLOCK)
            x = dot_nt(kx[at, :], q_t) * (SCALE * LOG2E) + shift
            if j == 2 * t + 1:
                x = jnp.where(first, x, NEG)
            p = jnp.exp2(x)
            dsb[at, cols] = (p * (dot_nt(vx[at, :], do_t) - delta)).astype(BF16)
            pb[at, cols] = p.astype(BF16)
    for j in range(0, CHIP_BLOCKS):
        at = slice(j * BLOCK, (j + 1) * BLOCK)
        upto = (j + 1) // 2 * TILE
        for n, (low, rows, by) in enumerate(((dsb, qs, SCALE), (pb, dos, 1.0))):
            value = dkv[n, at, :]
            if upto:
                value = value + dot_nn(low[at, :upto], rows[:upto, :])
            out[n, at, :] = value * by


def later(sc, off, own, recv, qd, stat, dkv):
    width = own.shape[2]
    heads = width // HDIM
    pair = pl.BlockSpec((2, OWN // 2, HDIM), lambda h, sc, off: (1, 0, h))
    full = pl.BlockSpec((2, OWN, HDIM), lambda h, sc, off: (0, 0, h))
    return pl.pallas_call(
        later_kernel,
        grid_spec=pltpu.PrefetchScalarGridSpec(
            num_scalar_prefetch=2,
            grid=(heads,),
            in_specs=[
                pair,
                pair,
                pl.BlockSpec((2, HALO, HDIM), lambda h, sc, off: (0, 0, h)),
                pl.BlockSpec((1, 8, OWN), lambda h, sc, off: (h, 0, 0)),
                full,
            ],
            out_specs=full,
            scratch_shapes=[pltpu.VMEM((OWN, HDIM), BF16)] * 4 + [pltpu.VMEM((OWN, OWN), BF16)] * 2,
        ),
        out_shape=jax.ShapeDtypeStruct((2, OWN, width), F32),
        compiler_params=params(),
        cost_estimate=cost(heads * 28 * 8 * 128**3 * 2, heads * 4_000_000),
        name="later",
    )(sc, off, own, recv, qd, stat, dkv)


def attn(sc, off, own, recv, halo, sums, base):
    width = own.shape[2]
    heads = width // HDIM
    keys = EXT + NSUM * BLOCK

    def by_head(n, rows):
        return pl.BlockSpec((n, rows, HDIM), lambda h, sc, off: (0, 0, h))

    sum_spec = pl.BlockSpec((2, BLOCK, HDIM), lambda h, sc, off: (0, 0, base + h))
    return pl.pallas_call(
        attn_kernel,
        grid_spec=pltpu.PrefetchScalarGridSpec(
            num_scalar_prefetch=2,
            grid=(heads,),
            in_specs=[by_head(4, OWN // 2), by_head(4, OWN // 2), by_head(2, HALO)]
            + [sum_spec] * NSUM,
            out_specs=[
                pl.BlockSpec((OWN, HDIM), lambda h, sc, off: (0, h)),
                by_head(2, OWN),
                pl.BlockSpec((1, 8, OWN), lambda h, sc, off: (h, 0, 0)),
                by_head(2, NSUM * BLOCK),
            ],
            scratch_shapes=[
                pltpu.VMEM((keys, HDIM), BF16),
                pltpu.VMEM((keys, HDIM), BF16),
                pltpu.VMEM((OWN, HDIM), BF16),
                pltpu.VMEM((OWN, HDIM), BF16),
                pltpu.VMEM((HDIM, keys), BF16),
                pltpu.VMEM((ROWS, TILE), F32),
                pltpu.VMEM((ROWS, TILE), F32),
                pltpu.VMEM((keys, OWN), BF16),
                pltpu.VMEM((OWN + NSUM * BLOCK, OWN), BF16),
            ],
        ),
        out_shape=[
            jax.ShapeDtypeStruct((OWN, width), BF16),
            jax.ShapeDtypeStruct((2, OWN, width), F32),
            jax.ShapeDtypeStruct((heads, 8, OWN), F32),
            jax.ShapeDtypeStruct((2, NSUM * BLOCK, width), BF16),
        ],
        compiler_params=params(),
        cost_estimate=cost(heads * 96 * 10 * 128**3 * 2, heads * 4_000_000),
        name="attn",
    )(sc, off, own, recv, halo, *sums)


def finish_kernel(sc, off, dq, dkv, *refs):
    tots, outs = refs[:SIDE], refs[SIDE:]
    core, y, z, x = sc[1], sc[2], sc[3], sc[4]
    local = off[y] & 7
    here = (off[y] >> 3) == z
    total = tots[0][...].astype(F32)
    for part in tots[1:]:
        total = total + part[...].astype(F32)
    for step in range(SIDE):
        for side in range(2):
            block = ((core + side) & 1) * SIDE + ((x + step) & 3)
            rows = pl.ds(pl.multiple_of(block * BLOCK, BLOCK), BLOCK)
            value = dkv[:, rows, :] + jnp.where(here & (local == block), total, 0.0)
            outs[step][side, 0] = dq[rows, :]
            outs[step][side, 1:3] = value.astype(BF16)


def finish(sc, off, dq, dkv, tots):
    width = dq.shape[1]
    shape = (2, 3, BLOCK, width)
    return pl.pallas_call(
        finish_kernel,
        grid_spec=pltpu.PrefetchScalarGridSpec(
            num_scalar_prefetch=2,
            grid=(width // HDIM,),
            in_specs=[
                pl.BlockSpec((OWN, HDIM), lambda h, sc, off: (0, h)),
                pl.BlockSpec((2, OWN, HDIM), lambda h, sc, off: (0, 0, h)),
            ]
            + [pl.BlockSpec((2, BLOCK, HDIM), lambda h, sc, off: (0, 0, h))] * SIDE,
            out_specs=[pl.BlockSpec((2, 3, BLOCK, HDIM), lambda h, sc, off: (0, 0, 0, h))] * SIDE,
        ),
        out_shape=[jax.ShapeDtypeStruct(shape, BF16)] * SIDE,
        compiler_params=params(),
        cost_estimate=cost(0, 20 * OWN * width),
        name="finish",
    )(sc, off, dq, dkv, *tots)


def place_kernel(sc, off, *refs):
    groups = len(SIZES)
    outs = refs[(SIDE + 1) * groups :]
    x, core = sc[4], sc[1]
    heads = sum(SIZES)
    at = 0
    for g in range(groups):
        width = SIZES[g] * HDIM
        for step in range(SIDE):
            source = (x + SIDE - step) & 3
            for part in range(2):
                side = core if part == 0 else 1 - core
                first = pl.multiple_of(((source * 2 + side) * heads + at) * HDIM, HDIM)
                ref = refs[g * (SIDE + 1) + (step if part == 0 else SIDE)]
                for n in range(3):
                    outs[n][:, pl.ds(first, width)] = ref[0 if part == 0 else step, n]
        at += SIZES[g]


def place(sc, off, parts):
    columns = sum(SIZES) * HDIM * 2 * SIDE
    shape = (BLOCK, columns)
    specs = []
    for n, p in enumerate(parts):
        lead = SIDE if n % (SIDE + 1) == SIDE else 1
        specs.append(pl.BlockSpec((lead, *p.shape[1:]), lambda i, sc, off: (0, 0, 0, 0)))
    return pl.pallas_call(
        place_kernel,
        grid_spec=pltpu.PrefetchScalarGridSpec(
            num_scalar_prefetch=2,
            grid=(1,),
            in_specs=specs,
            out_specs=[whole(shape)] * 3,
        ),
        out_shape=[jax.ShapeDtypeStruct(shape, BF16)] * 3,
        compiler_params=params(),
        cost_estimate=cost(0, 12 * BLOCK * columns),
        name="place",
    )(sc, off, *parts)


def named(value, pairs, axis="ctx"):
    return lax.ppermute(value, axis, pairs)


def on_device(query, key_in, value_in, dout, off):
    width = query.shape[1]
    me = lax.axis_index("ctx")
    x = lax.axis_index("tp")
    which = lax.iota(jnp.int32, 8)
    sc = jnp.where(which == 0, me >> 1, me & 1)
    sc = jnp.where(which == 2, me >> 3, sc)
    sc = jnp.where(which == 3, (me >> 1) & 3, sc)
    sc = jnp.where(which == 4, x, sc).astype(jnp.int32)
    y, z = me >> 3, (me >> 1) & 3

    own_cand, oth_cand = candidate(sc, off, key_in, value_in)
    pieces = pieces_of(sc, off, own_cand, named(oth_cand, SWAP))
    arrived = [pieces[0]]
    arrived += [named(pieces[n], along_z(n)) for n in range(1, SIDE)]
    step = (z - (off[y] >> 3)) & 3
    piece = arrived[0]
    for n in range(1, SIDE):
        piece = jnp.where(step == n, arrived[n], piece)
    parts = [piece] + [named(piece, along_z(n)) for n in range(1, SIDE)]
    summary = gather(sc, off, parts)
    sums = [summary] + [named(summary, along_y(n)) for n in range(1, NSUM)]

    bases = [sum(SIZES[:g]) for g in range(len(SIZES))]
    work = []
    for g, heads in enumerate(SIZES):
        own, oth = pack(sc, off, (query, dout, key_in, value_in), bases[g], heads, width)
        recv = named(oth, SWAP)
        qd, kv = halo_of(sc, off, own, recv)
        work.append((own, recv, named(kv, ring(1)), named(qd, ring(-1))))

    parts = []
    for g, heads in enumerate(SIZES):
        own, recv, kv, qd = work[g]
        dq, dkv, stat, sent = attn(sc, off, own, recv, kv, sums, bases[g])
        stat = named(stat, ring(-1))
        dkv = later(sc, off, own, recv, qd, stat, dkv)
        part = sent[:, :BLOCK].astype(F32)
        for n in range(1, NSUM):
            moved = named(sent[:, n * BLOCK : (n + 1) * BLOCK], along_y(-n))
            part = part + moved.astype(F32)
        part = part.astype(BF16)
        tots = [part] + [named(part, along_z(n)) for n in range(1, SIDE)]
        cuts = finish(sc, off, dq, dkv, tots)
        there = [cuts[0]]
        there += [named(cuts[n], along_x(n), "tp") for n in range(1, SIDE)]
        parts += there
        parts.append(named(jnp.concatenate([t[1:] for t in there], axis=0), SWAP))
    return tuple(place(sc, off, parts))


def solution(mesh):
    return jax.shard_map(
        on_device,
        mesh=mesh,
        in_specs=(P("ctx", "tp"), P("ctx", "tp"), P("ctx", "tp"), P("ctx", "tp"), P()),
        out_specs=(P(("ctx", "tp"), None),) * 3,
        check_vma=False,
    )
```

profile of v0, /device:TPU:8, one launch (start us, length us, event | category | flops | bytes accessed | tf_op | source)
XLA Modules:
  0.0 249.0 jit_solution(3396337298499219704)
XLA Ops:
  1.2 4.0 %pack.3 = (bf16[4,512,384]{2,1,0:T(8,128)(2,1)}, bf16[4,512,384]{2,1,0:T(8,128)(2,1)}) custom-call(s32[8]{0:T(128)} %compare_select_fusion.3.sc, s32[4]{0:T(128)} %off.27, bf16[512,1536]{1,0:T(8,128)(2,1)} %refs_1_.3, bf16[512,1536]{1,0:T(8,128)(2,1)} %refs_1_.3, bf16[512,1536]{1,0:T(8,128)(2,1)} %refs_3_.3, bf16[512,1536]{1,0:T(8,128)(2,1)} %refs_3_.3, ...), custom_call_target="tpu_custom_call" | custom-call | bytes 6291456 | tf_op jit(solution)/shard_map/pack/pallas_call | solution.py:102
  5.2 4.0 %pack.2 = (bf16[4,512,384]{2,1,0:T(8,128)(2,1)}, bf16[4,512,384]{2,1,0:T(8,128)(2,1)}) custom-call(s32[8]{0:T(128)} %compare_select_fusion.3.sc, s32[4]{0:T(128)} %off.27, bf16[512,1536]{1,0:T(8,128)(2,1)} %refs_1_.3, bf16[512,1536]{1,0:T(8,128)(2,1)} %refs_1_.3, bf16[512,1536]{1,0:T(8,128)(2,1)} %refs_3_.3, bf16[512,1536]{1,0:T(8,128)(2,1)} %refs_3_.3, ...), custom_call_target="tpu_custom_call" | custom-call | bytes 6291456 | tf_op jit(solution)/shard_map/pack/pallas_call | solution.py:102
  10.9 5.1 %halo.3 = (bf16[2,896,384]{2,1,0:T(8,128)(2,1)}, bf16[2,896,384]{2,1,0:T(8,128)(2,1)}) custom-call(s32[8]{0:T(128)} %compare_select_fusion.3.sc, s32[4]{0:T(128)} %off.27, bf16[4,512,384]{2,1,0:T(8,128)(2,1)} %get-tuple-element.51.own, bf16[4,512,384]{2,1,0:T(8,128)(2,1)} %copy-done.1), custom_call_target="tpu_custom_call" | custom-call | bytes 12582912 | tf_op jit(solution)/shard_map/halo/pallas_call | solution.py:138
  17.9 2.8 %candidate.1 = (bf16[2,128,768]{2,1,0:T(8,128)(2,1)}, bf16[2,128,768]{2,1,0:T(8,128)(2,1)}) custom-call(s32[8]{0:T(128)} %compare_select_fusion.3.sc, s32[4]{0:T(128)} %off.27, bf16[512,1536]{1,0:T(8,128)(2,1)} %refs_5_.3, bf16[512,1536]{1,0:T(8,128)(2,1)} %refs_7_.3), custom_call_target="tpu_custom_call" | custom-call | bytes 1572864 | tf_op jit(solution)/shard_map/candidate/pallas_call | solution.py:167
  32.3 22.5 %collective-permute-done.4 = bf16[2,32,768]{2,1,0:T(8,128)(2,1)S(1)} collective-permute-done((bf16[2,32,768]{2,1,0:T(8,128)(2,1)}, bf16[2,32,768]{2,1,0:T(8,128)(2,1)S(1)}, u32[]{:S(2)}, u32[]{:S(2)}) %collective-permute-start.4) | collective-permute-done | bytes 98336 | tf_op jit(solution)/shard_map/ppermute | solution.py:531
  55.8 3.2 %collective-permute-start.7 = (bf16[2,32,768]{2,1,0:T(8,128)(2,1)S(1)}, bf16[2,32,768]{2,1,0:T(8,128)(2,1)S(1)}, u32[]{:S(2)}, u32[]{:S(2)}) collective-permute-start(bf16[2,32,768]{2,1,0:T(8,128)(2,1)S(1)} %select_select_fusion.refs_0_), channel_id=1, source_target_pairs={{0,16},{4,20},{8,24},{12,28},{16,0},{20,4},{24,8},{28,12},{32,48},... | collective-permute-start | bytes 294920 | tf_op jit(solution)/shard_map/ppermute | solution.py:531
  59.1 4.3 %collective-permute-done.6.refs_1_ = bf16[2,32,768]{2,1,0:T(8,128)(2,1)S(1)} collective-permute-done((bf16[2,32,768]{2,1,0:T(8,128)(2,1)S(1)}, bf16[2,32,768]{2,1,0:T(8,128)(2,1)S(1)}, u32[]{:S(2)}, u32[]{:S(2)}) %collective-permute-start.6) | collective-permute-done | bytes 98336 | tf_op jit(solution)/shard_map/ppermute | solution.py:531
  72.0 2.9 %collective-permute-start.26 = (bf16[2,896,384]{2,1,0:T(8,128)(2,1)}, bf16[2,896,384]{2,1,0:T(8,128)(2,1)S(1)}, u32[]{:S(2)}, u32[]{:S(2)}) collective-permute-start(bf16[2,896,384]{2,1,0:T(8,128)(2,1)} %get-tuple-element.55), channel_id=1, source_target_pairs={{0,120},{4,124},{8,0},{12,4},{16,8},{20,12},{24,16},{28,20},{32,24... | collective-permute-start | bytes 4128776 | tf_op jit(solution)/shard_map/ppermute | solution.py:531
  74.9 5.1 %halo.2 = (bf16[2,896,384]{2,1,0:T(8,128)(2,1)}, bf16[2,896,384]{2,1,0:T(8,128)(2,1)}) custom-call(s32[8]{0:T(128)} %compare_select_fusion.3.sc, s32[4]{0:T(128)} %off.27, bf16[4,512,384]{2,1,0:T(8,128)(2,1)} %get-tuple-element.33.own, bf16[4,512,384]{2,1,0:T(8,128)(2,1)} %copy-done), custom_call_target="tpu_custom_call" | custom-call | bytes 12582912 | tf_op jit(solution)/shard_map/halo/pallas_call | solution.py:138
  81.6 5.9 %collective-permute-done.11.s3 = bf16[2,128,768]{2,1,0:T(8,128)(2,1)S(1)} collective-permute-done((bf16[2,128,768]{2,1,0:T(8,128)(2,1)}, bf16[2,128,768]{2,1,0:T(8,128)(2,1)S(1)}, u32[]{:S(2)}, u32[]{:S(2)}) %collective-permute-start.11) | collective-permute-done | bytes 393248 | tf_op jit(solution)/shard_map/ppermute | solution.py:531
  91.0 18.9 %attn.3 = (bf16[1024,384]{1,0:T(8,128)(2,1)}, f32[2,1024,384]{2,1,0:T(8,128)}, f32[3,8,1024]{2,1,0:T(8,128)}, bf16[2,512,384]{2,1,0:T(8,128)(2,1)}) custom-call(s32[8]{0:T(128)} %compare_select_fusion.3.sc, s32[4]{0:T(128)} %off.27, bf16[4,512,384]{2,1,0:T(8,128)(2,1)} %get-tuple-element.51.own, bf16[4,512,384]{2,1,0:T(8,128)(2,1)} %copy-done.1, ...), custom_call_target="tpu_custom_call" | custom-call | flops 12079595520 | bytes 12000000 | tf_op jit(solution)/shard_map/attn/pallas_call | solution.py:413
  114.1 6.9 %collective-permute-done.1.halo = bf16[2,896,384]{2,1,0:T(8,128)(2,1)S(1)} collective-permute-done((bf16[2,896,384]{2,1,0:T(8,128)(2,1)}, bf16[2,896,384]{2,1,0:T(8,128)(2,1)S(1)}, u32[]{:S(2)}, u32[]{:S(2)}) %collective-permute-start.1) | collective-permute-done | bytes 1376288 | tf_op jit(solution)/shard_map/ppermute | solution.py:531
  122.4 19.0 %attn.2 = (bf16[1024,384]{1,0:T(8,128)(2,1)}, f32[2,1024,384]{2,1,0:T(8,128)}, f32[3,8,1024]{2,1,0:T(8,128)}, bf16[2,512,384]{2,1,0:T(8,128)(2,1)}) custom-call(s32[8]{0:T(128)} %compare_select_fusion.3.sc, s32[4]{0:T(128)} %off.27, bf16[4,512,384]{2,1,0:T(8,128)(2,1)} %get-tuple-element.33.own, bf16[4,512,384]{2,1,0:T(8,128)(2,1)} %copy-done, ...), custom_call_target="tpu_custom_call" | custom-call | flops 12079595520 | bytes 12000000 | tf_op jit(solution)/shard_map/attn/pallas_call | solution.py:413
  141.4 10.8 %collective-permute-done.28 = bf16[2,128,384]{2,1,0:T(8,128)(2,1)S(1)} collective-permute-done((bf16[2,128,384]{2,1,0:T(8,128)(2,1)S(1)}, bf16[2,128,384]{2,1,0:T(8,128)(2,1)S(1)}, u32[]{:S(2)}, u32[]{:S(2)}) %collective-permute-start.28) | collective-permute-done | bytes 196640 | tf_op jit(solution)/shard_map/ppermute | solution.py:531
  159.2 6.4 %collective-permute-done.31.refs_1_ = bf16[2,128,384]{2,1,0:T(8,128)(2,1)S(1)} collective-permute-done((bf16[2,128,384]{2,1,0:T(8,128)(2,1)S(1)}, bf16[2,128,384]{2,1,0:T(8,128)(2,1)S(1)}, u32[]{:S(2)}, u32[]{:S(2)}) %collective-permute-start.31) | collective-permute-done | bytes 196640 | tf_op jit(solution)/shard_map/ppermute | solution.py:531
  166.0 7.8 %later.3.dkv = f32[2,1024,384]{2,1,0:T(8,128)} custom-call(s32[8]{0:T(128)} %compare_select_fusion.3.sc, s32[4]{0:T(128)} %off.27, bf16[4,512,384]{2,1,0:T(8,128)(2,1)} %get-tuple-element.51.own, bf16[4,512,384]{2,1,0:T(8,128)(2,1)} %copy-done.1, bf16[2,896,384]{2,1,0:T(8,128)(2,1)} %copy-done.3, f32[3,8,1024]{2,1,0:T(8,128)} %copy-done.24, ...), custom_call_target="tpu_custom_call" | custom-call | flops 2818572288 | bytes 12000000 | tf_op jit(solution)/shard_map/later/pallas_call | solution.py:382
  174.6 5.2 %finish.3 = (bf16[2,3,128,384]{3,2,1,0:T(8,128)(2,1)}, bf16[2,3,128,384]{3,2,1,0:T(8,128)(2,1)}, bf16[2,3,128,384]{3,2,1,0:T(8,128)(2,1)}, bf16[2,3,128,384]{3,2,1,0:T(8,128)(2,1)}) custom-call(s32[8]{0:T(128)} %compare_select_fusion.3.sc, s32[4]{0:T(128)} %off.27, bf16[1024,384]{1,0:T(8,128)(2,1)} %get-tuple-element.54.dq, f32[2,1024,384]{2,1,0:T(8,128)} %later.3.dkv, ...), custom_call_target="tpu_custom_call" | custom-call | bytes 7864320 | tf_op jit(solution)/shard_map/finish/pallas_call | solution.py:470
  193.1 7.8 %later.2.dkv = f32[2,1024,384]{2,1,0:T(8,128)} custom-call(s32[8]{0:T(128)} %compare_select_fusion.3.sc, s32[4]{0:T(128)} %off.27, bf16[4,512,384]{2,1,0:T(8,128)(2,1)} %get-tuple-element.33.own, bf16[4,512,384]{2,1,0:T(8,128)(2,1)} %copy-done, bf16[2,896,384]{2,1,0:T(8,128)(2,1)} %copy-done.2, f32[3,8,1024]{2,1,0:T(8,128)} %copy-done.25, ...), custom_call_target="tpu_custom_call" | custom-call | flops 2818572288 | bytes 12000000 | tf_op jit(solution)/shard_map/later/pallas_call | solution.py:382
  201.7 5.1 %finish.2 = (bf16[2,3,128,384]{3,2,1,0:T(8,128)(2,1)}, bf16[2,3,128,384]{3,2,1,0:T(8,128)(2,1)}, bf16[2,3,128,384]{3,2,1,0:T(8,128)(2,1)}, bf16[2,3,128,384]{3,2,1,0:T(8,128)(2,1)}) custom-call(s32[8]{0:T(128)} %compare_select_fusion.3.sc, s32[4]{0:T(128)} %off.27, bf16[1024,384]{1,0:T(8,128)(2,1)} %get-tuple-element.42.dq, f32[2,1024,384]{2,1,0:T(8,128)} %later.2.dkv, ...), custom_call_target="tpu_custom_call" | custom-call | bytes 7864320 | tf_op jit(solution)/shard_map/finish/pallas_call | solution.py:470
  211.3 7.2 %collective-permute-done.36.refs_8_ = bf16[2,3,128,384]{3,2,1,0:T(8,128)(2,1)S(1)} collective-permute-done((bf16[2,3,128,384]{3,2,1,0:T(8,128)(2,1)}, bf16[2,3,128,384]{3,2,1,0:T(8,128)(2,1)S(1)}, u32[]{:S(2)}, u32[]{:S(2)}) %collective-permute-start.36) | collective-permute-done | bytes 589856 | tf_op jit(solution)/shard_map/ppermute | solution.py:531
  219.4 14.5 %collective-permute-done.20.refs_1_ = bf16[2,3,128,384]{3,2,1,0:T(8,128)(2,1)S(1)} collective-permute-done((bf16[2,3,128,384]{3,2,1,0:T(8,128)(2,1)}, bf16[2,3,128,384]{3,2,1,0:T(8,128)(2,1)S(1)}, u32[]{:S(2)}, u32[]{:S(2)}) %collective-permute-start.20) | collective-permute-done | bytes 589856 | tf_op jit(solution)/shard_map/ppermute | solution.py:531
  233.9 4.7 %collective-permute-done.22.refs_3_ = bf16[2,3,128,384]{3,2,1,0:T(8,128)(2,1)S(1)} collective-permute-done((bf16[2,3,128,384]{3,2,1,0:T(8,128)(2,1)}, bf16[2,3,128,384]{3,2,1,0:T(8,128)(2,1)S(1)}, u32[]{:S(2)}, u32[]{:S(2)}) %collective-permute-start.22) | collective-permute-done | bytes 589856 | tf_op jit(solution)/shard_map/ppermute | solution.py:531
  239.5 2.8 %collective-permute-done.23.refs_4_ = bf16[4,3,128,384]{3,2,1,0:T(8,128)(2,1)S(1)} collective-permute-done((bf16[4,3,128,384]{3,2,1,0:T(8,128)(2,1)S(1)}, bf16[4,3,128,384]{3,2,1,0:T(8,128)(2,1)S(1)}, u32[]{:S(2)}, u32[]{:S(2)}) %collective-permute-start.23) | collective-permute-done | bytes 1179680 | tf_op jit(solution)/shard_map/ppermute | solution.py:531
  243.3 5.7 %place.1 = (bf16[128,6144]{1,0:T(8,128)(2,1)}, bf16[128,6144]{1,0:T(8,128)(2,1)}, bf16[128,6144]{1,0:T(8,128)(2,1)}) custom-call(s32[8]{0:T(128)} %compare_select_fusion.3.sc, s32[4]{0:T(128)} %off.27, bf16[2,3,128,384]{3,2,1,0:T(8,128)(2,1)} %get-tuple-element.47.refs_0_, bf16[2,3,128,384]{3,2,1,0:T(8,128)(2,1)} %copy-done.8, ...), custom_call_target="tpu_custom_call" | custom-call | bytes 9437184 | tf_op jit(solution)/shard_map/place/pallas_call | solution.py:515
  (155 shorter events, 64.6 us)
Async XLA Ops:
  9.3 62.8 %collective-permute-start = (bf16[4,512,384]{2,1,0:T(8,128)(2,1)}, bf16[4,512,384]{2,1,0:T(8,128)(2,1)S(1)}, u32[]{:S(2)}, u32[]{:S(2)}) collective-permute-start(bf16[4,512,384]{2,1,0:T(8,128)(2,1)} %get-tuple-element.34), channel_id=1, source_target_pairs={{0,4},{4,0},{8,12},{12,8},{16,20},{20,16},{24,28},{28,24},{32,36},... | collective-permute-start | bytes 4718600 | tf_op jit(solution)/shard_map/ppermute | solution.py:531
  16.0 74.2 %collective-permute-start.25 = (bf16[2,896,384]{2,1,0:T(8,128)(2,1)}, bf16[2,896,384]{2,1,0:T(8,128)(2,1)}, u32[]{:S(2)}, u32[]{:S(2)}) collective-permute-start(bf16[2,896,384]{2,1,0:T(8,128)(2,1)} %get-tuple-element.53), channel_id=1, source_target_pairs={{0,8},{4,12},{8,16},{12,20},{16,24},{20,28},{24,32},{28,36},{32,40... | collective-permute-start | bytes 4128776 | tf_op jit(solution)/shard_map/ppermute | solution.py:531
  28.3 26.6 %collective-permute-start.4 = (bf16[2,32,768]{2,1,0:T(8,128)(2,1)}, bf16[2,32,768]{2,1,0:T(8,128)(2,1)S(1)}, u32[]{:S(2)}, u32[]{:S(2)}) collective-permute-start(bf16[2,32,768]{2,1,0:T(8,128)(2,1)} %get-tuple-element.39), channel_id=1, source_target_pairs={{0,16},{4,20},{8,24},{12,28},{16,0},{20,4},{24,8},{28,12},{32,48},... | collective-permute-start | bytes 294920 | tf_op jit(solution)/shard_map/ppermute | solution.py:531
  29.9 24.9 %collective-permute-start.5 = (bf16[2,32,768]{2,1,0:T(8,128)(2,1)}, bf16[2,32,768]{2,1,0:T(8,128)(2,1)S(1)}, u32[]{:S(2)}, u32[]{:S(2)}) collective-permute-start(bf16[2,32,768]{2,1,0:T(8,128)(2,1)} %get-tuple-element.40), channel_id=1, source_target_pairs={{0,8},{4,12},{8,16},{12,20},{16,24},{20,28},{24,0},{28,4},{32,40},... | collective-permute-start | bytes 294920 | tf_op jit(solution)/shard_map/ppermute | solution.py:531
  69.2 18.3 %collective-permute-start.11 = (bf16[2,128,768]{2,1,0:T(8,128)(2,1)}, bf16[2,128,768]{2,1,0:T(8,128)(2,1)S(1)}, u32[]{:S(2)}, u32[]{:S(2)}) collective-permute-start(bf16[2,128,768]{2,1,0:T(8,128)(2,1)} %gather.1.s0), channel_id=1, source_target_pairs={{0,96},{4,100},{8,104},{12,108},{16,112},{20,116},{24,120},{28,124... | collective-permute-start | bytes 1179656 | tf_op jit(solution)/shard_map/ppermute | solution.py:531
  70.9 19.3 %collective-permute-start.9 = (bf16[2,128,768]{2,1,0:T(8,128)(2,1)}, bf16[2,128,768]{2,1,0:T(8,128)(2,1)S(1)}, u32[]{:S(2)}, u32[]{:S(2)}) collective-permute-start(bf16[2,128,768]{2,1,0:T(8,128)(2,1)} %gather.1.s0), channel_id=1, source_target_pairs={{0,32},{4,36},{8,40},{12,44},{16,48},{20,52},{24,56},{28,60},{32,6... | collective-permute-start | bytes 1179656 | tf_op jit(solution)/shard_map/ppermute | solution.py:531
  72.0 83.8 %collective-permute-start.26 = (bf16[2,896,384]{2,1,0:T(8,128)(2,1)}, bf16[2,896,384]{2,1,0:T(8,128)(2,1)S(1)}, u32[]{:S(2)}, u32[]{:S(2)}) collective-permute-start(bf16[2,896,384]{2,1,0:T(8,128)(2,1)} %get-tuple-element.55), channel_id=1, source_target_pairs={{0,120},{4,124},{8,0},{12,4},{16,8},{20,12},{24,16},{28,20},{32,24... | collective-permute-start | bytes 4128776 | tf_op jit(solution)/shard_map/ppermute | solution.py:531
  81.0 40.0 %collective-permute-start.1 = (bf16[2,896,384]{2,1,0:T(8,128)(2,1)}, bf16[2,896,384]{2,1,0:T(8,128)(2,1)S(1)}, u32[]{:S(2)}, u32[]{:S(2)}) collective-permute-start(bf16[2,896,384]{2,1,0:T(8,128)(2,1)} %get-tuple-element.35), channel_id=1, source_target_pairs={{0,8},{4,12},{8,16},{12,20},{16,24},{20,28},{24,32},{28,36},{32,40... | collective-permute-start | bytes 4128776 | tf_op jit(solution)/shard_map/ppermute | solution.py:531
  87.5 98.3 %collective-permute-start.12 = (bf16[2,896,384]{2,1,0:T(8,128)(2,1)}, bf16[2,896,384]{2,1,0:T(8,128)(2,1)S(1)}, u32[]{:S(2)}, u32[]{:S(2)}) collective-permute-start(bf16[2,896,384]{2,1,0:T(8,128)(2,1)} %get-tuple-element.43), channel_id=1, source_target_pairs={{0,120},{4,124},{8,0},{12,4},{16,8},{20,12},{24,16},{28,20},{32,24... | collective-permute-start | bytes 4128776 | tf_op jit(solution)/shard_map/ppermute | solution.py:531
  111.0 41.2 %collective-permute-start.28 = (bf16[2,128,384]{2,1,0:T(8,128)(2,1)S(1)}, bf16[2,128,384]{2,1,0:T(8,128)(2,1)S(1)}, u32[]{:S(2)}, u32[]{:S(2)}) collective-permute-start(bf16[2,128,384]{2,1,0:T(8,128)(2,1)S(1)} %get-tuple-element.63), channel_id=1, source_target_pairs={{0,96},{4,100},{8,104},{12,108},{16,112},{20,116},{24,120},{28,124... | collective-permute-start | bytes 589832 | tf_op jit(solution)/shard_map/ppermute | solution.py:531
  113.7 40.8 %collective-permute-start.29 = (bf16[2,128,384]{2,1,0:T(8,128)(2,1)S(1)}, bf16[2,128,384]{2,1,0:T(8,128)(2,1)S(1)}, u32[]{:S(2)}, u32[]{:S(2)}) collective-permute-start(bf16[2,128,384]{2,1,0:T(8,128)(2,1)S(1)} %get-tuple-element.65), channel_id=1, source_target_pairs={{0,64},{4,68},{8,72},{12,76},{16,80},{20,84},{24,88},{28,92},{32,9... | collective-permute-start | bytes 589832 | tf_op jit(solution)/shard_map/ppermute | solution.py:531
  121.0 33.5 %collective-permute-start.30 = (bf16[2,128,384]{2,1,0:T(8,128)(2,1)S(1)}, bf16[2,128,384]{2,1,0:T(8,128)(2,1)S(1)}, u32[]{:S(2)}, u32[]{:S(2)}) collective-permute-start(bf16[2,128,384]{2,1,0:T(8,128)(2,1)S(1)} %get-tuple-element.64), channel_id=1, source_target_pairs={{0,32},{4,36},{8,40},{12,44},{16,48},{20,52},{24,56},{28,60},{32,6... | collective-permute-start | bytes 589832 | tf_op jit(solution)/shard_map/ppermute | solution.py:531
  155.8 25.5 %collective-permute-start.14 = (bf16[2,128,384]{2,1,0:T(8,128)(2,1)S(1)}, bf16[2,128,384]{2,1,0:T(8,128)(2,1)S(1)}, u32[]{:S(2)}, u32[]{:S(2)}) collective-permute-start(bf16[2,128,384]{2,1,0:T(8,128)(2,1)S(1)} %get-tuple-element.66), channel_id=1, source_target_pairs={{0,96},{4,100},{8,104},{12,108},{16,112},{20,116},{24,120},{28,124... | collective-permute-start | bytes 589832 | tf_op jit(solution)/shard_map/ppermute | solution.py:531
  157.0 24.3 %collective-permute-start.15 = (bf16[2,128,384]{2,1,0:T(8,128)(2,1)S(1)}, bf16[2,128,384]{2,1,0:T(8,128)(2,1)S(1)}, u32[]{:S(2)}, u32[]{:S(2)}) collective-permute-start(bf16[2,128,384]{2,1,0:T(8,128)(2,1)S(1)} %get-tuple-element.68), channel_id=1, source_target_pairs={{0,64},{4,68},{8,72},{12,76},{16,80},{20,84},{24,88},{28,92},{32,9... | collective-permute-start | bytes 589832 | tf_op jit(solution)/shard_map/ppermute | solution.py:531
  165.6 15.7 %collective-permute-start.16 = (bf16[2,128,384]{2,1,0:T(8,128)(2,1)S(1)}, bf16[2,128,384]{2,1,0:T(8,128)(2,1)S(1)}, u32[]{:S(2)}, u32[]{:S(2)}) collective-permute-start(bf16[2,128,384]{2,1,0:T(8,128)(2,1)S(1)} %get-tuple-element.67), channel_id=1, source_target_pairs={{0,32},{4,36},{8,40},{12,44},{16,48},{20,52},{24,56},{28,60},{32,6... | collective-permute-start | bytes 589832 | tf_op jit(solution)/shard_map/ppermute | solution.py:531
  179.8 28.6 %collective-permute-start.34 = (bf16[2,3,128,384]{3,2,1,0:T(8,128)(2,1)}, bf16[2,3,128,384]{3,2,1,0:T(8,128)(2,1)S(1)}, u32[]{:S(2)}, u32[]{:S(2)}) collective-permute-start(bf16[2,3,128,384]{3,2,1,0:T(8,128)(2,1)} %get-tuple-element.60), channel_id=1, source_target_pairs={{0,1},{1,2},{2,3},{3,0},{4,5},{5,6},{6,7},{7,4},{8,9},{9,10},{10,1... | collective-permute-start | bytes 1769480 | tf_op jit(solution)/shard_map/ppermute | solution.py:531
  185.8 15.1 %collective-permute-start.18 = (bf16[2,128,384]{2,1,0:T(8,128)(2,1)S(1)}, bf16[2,128,384]{2,1,0:T(8,128)(2,1)S(1)}, u32[]{:S(2)}, u32[]{:S(2)}) collective-permute-start(bf16[2,128,384]{2,1,0:T(8,128)(2,1)S(1)} %add_convert_fusion.1.refs_0_), channel_id=1, source_target_pairs={{0,16},{4,20},{8,24},{12,28},{16,0},{20,4},{24,8},{28,12},{32,48},... | collective-permute-start | bytes 589832 | tf_op jit(solution)/shard_map/ppermute | solution.py:531
  185.9 15.1 %collective-permute-start.19 = (bf16[2,128,384]{2,1,0:T(8,128)(2,1)S(1)}, bf16[2,128,384]{2,1,0:T(8,128)(2,1)S(1)}, u32[]{:S(2)}, u32[]{:S(2)}) collective-permute-start(bf16[2,128,384]{2,1,0:T(8,128)(2,1)S(1)} %add_convert_fusion.1.refs_0_), channel_id=1, source_target_pairs={{0,24},{4,28},{8,0},{12,4},{16,8},{20,12},{24,16},{28,20},{32,56},... | collective-permute-start | bytes 589832 | tf_op jit(solution)/shard_map/ppermute | solution.py:531
  188.9 22.4 %collective-permute-start.35 = (bf16[2,3,128,384]{3,2,1,0:T(8,128)(2,1)}, bf16[2,3,128,384]{3,2,1,0:T(8,128)(2,1)S(1)}, u32[]{:S(2)}, u32[]{:S(2)}) collective-permute-start(bf16[2,3,128,384]{3,2,1,0:T(8,128)(2,1)} %get-tuple-element.61), channel_id=1, source_target_pairs={{0,2},{1,3},{2,0},{3,1},{4,6},{5,7},{6,4},{7,5},{8,10},{9,11},{10,... | collective-permute-start | bytes 1769480 | tf_op jit(solution)/shard_map/ppermute | solution.py:531
  191.6 26.9 %collective-permute-start.36 = (bf16[2,3,128,384]{3,2,1,0:T(8,128)(2,1)}, bf16[2,3,128,384]{3,2,1,0:T(8,128)(2,1)S(1)}, u32[]{:S(2)}, u32[]{:S(2)}) collective-permute-start(bf16[2,3,128,384]{3,2,1,0:T(8,128)(2,1)} %get-tuple-element.62), channel_id=1, source_target_pairs={{0,3},{1,0},{2,1},{3,2},{4,7},{5,4},{6,5},{7,6},{8,11},{9,8},{10,9... | collective-permute-start | bytes 1769480 | tf_op jit(solution)/shard_map/ppermute | solution.py:531
  206.8 27.0 %collective-permute-start.20 = (bf16[2,3,128,384]{3,2,1,0:T(8,128)(2,1)}, bf16[2,3,128,384]{3,2,1,0:T(8,128)(2,1)S(1)}, u32[]{:S(2)}, u32[]{:S(2)}) collective-permute-start(bf16[2,3,128,384]{3,2,1,0:T(8,128)(2,1)} %get-tuple-element.48), channel_id=1, source_target_pairs={{0,1},{1,2},{2,3},{3,0},{4,5},{5,6},{6,7},{7,4},{8,9},{9,10},{10,1... | collective-permute-start | bytes 1769480 | tf_op jit(solution)/shard_map/ppermute | solution.py:531
  207.4 26.4 %collective-permute-start.21 = (bf16[2,3,128,384]{3,2,1,0:T(8,128)(2,1)}, bf16[2,3,128,384]{3,2,1,0:T(8,128)(2,1)S(1)}, u32[]{:S(2)}, u32[]{:S(2)}) collective-permute-start(bf16[2,3,128,384]{3,2,1,0:T(8,128)(2,1)} %get-tuple-element.49), channel_id=1, source_target_pairs={{0,2},{1,3},{2,0},{3,1},{4,6},{5,7},{6,4},{7,5},{8,10},{9,11},{10,... | collective-permute-start | bytes 1769480 | tf_op jit(solution)/shard_map/ppermute | solution.py:531
  208.3 30.3 %collective-permute-start.22 = (bf16[2,3,128,384]{3,2,1,0:T(8,128)(2,1)}, bf16[2,3,128,384]{3,2,1,0:T(8,128)(2,1)S(1)}, u32[]{:S(2)}, u32[]{:S(2)}) collective-permute-start(bf16[2,3,128,384]{3,2,1,0:T(8,128)(2,1)} %get-tuple-element.50), channel_id=1, source_target_pairs={{0,3},{1,0},{2,1},{3,2},{4,7},{5,4},{6,5},{7,6},{8,11},{9,8},{10,9... | collective-permute-start | bytes 1769480 | tf_op jit(solution)/shard_map/ppermute | solution.py:531
  219.4 20.1 %collective-permute-start.37 = (bf16[4,3,128,384]{3,2,1,0:T(8,128)(2,1)S(1)}, bf16[4,3,128,384]{3,2,1,0:T(8,128)(2,1)S(1)}, u32[]{:S(2)}, u32[]{:S(2)}) collective-permute-start(bf16[4,3,128,384]{3,2,1,0:T(8,128)(2,1)S(1)} %pad_maximum_fusion.1), channel_id=1, source_target_pairs={{0,4},{4,0},{8,12},{12,8},{16,20},{20,16},{24,28},{28,24},{32,36},... | collective-permute-start | bytes 3538952 | tf_op jit(solution)/shard_map/ppermute | solution.py:531
  (50 other events, 335.2 us)
where the time goes:
time: 252 us; the launch traced here: 249 us
  Pallas kernels  95.5 us (38%)
  waiting for transfers between devices  93.6 us (37%)
  starting transfers between devices  44.9 us (18%)
  local copies, waits for them, and re-layouts  10.1 us (4%)
  other arithmetic  3.02 us (1%)
    ppermute x38, waiting for transfers between devices, named(): return lax.ppermute(value, axis, pairs)  93.6 us
    ppermute x38, starting transfers between devices, named(): return lax.ppermute(value, axis, pairs)  44.9 us
    pallas_call x2, Pallas kernels, attn(): pl.pallas_call(attn_kernel, grid_spec=pltpu.PrefetchScalarGridSpec(num_sc...  37.9 us
    pallas_call x2, Pallas kernels, later(): pl.pallas_call(later_kernel, grid_spec=pltpu.PrefetchScalarGridSpec(num_s...  15.7 us
    pallas_call x2, Pallas kernels, finish(): pl.pallas_call(finish_kernel, grid_spec=pltpu.PrefetchScalarGridSpec(num_...  10.3 us
    pallas_call x2, Pallas kernels, halo_of(): pl.pallas_call(halo_kernel, grid_spec=pltpu.PrefetchScalarGridSpec(num_sc...  10.2 us
    pallas_call x2, Pallas kernels, pack(): pl.pallas_call(pack_kernel, grid_spec=pltpu.PrefetchScalarGridSpec(num_sc...  8.01 us
    unnamed x72, local copies, waits for them, and re-layouts  7 us
  transfers between devices with their start and end apart: 38, of which 16 were waited for; matrix products, arithmetic and copies ran while one was open for 2% of the time, Pallas kernels for 35%

commit v1 on v0

--- a/solution.py
+++ b/solution.py
@@ -447,7 +447,7 @@
     )(sc, off, own, recv, halo, *sums)
 
 
-def finish_kernel(sc, off, dq, dkv, *refs):
+def finish_kernel(sc, off, dkv, *refs):
     tots, outs = refs[:SIDE], refs[SIDE:]
     core, y, z, x = sc[1], sc[2], sc[3], sc[4]
     local = off[y] & 7
@@ -460,71 +460,102 @@
             block = ((core + side) & 1) * SIDE + ((x + step) & 3)
             rows = pl.ds(pl.multiple_of(block * BLOCK, BLOCK), BLOCK)
             value = dkv[:, rows, :] + jnp.where(here & (local == block), total, 0.0)
-            outs[step][side, 0] = dq[rows, :]
-            outs[step][side, 1:3] = value.astype(BF16)
-
-
-def finish(sc, off, dq, dkv, tots):
-    width = dq.shape[1]
-    shape = (2, 3, BLOCK, width)
+            outs[step][side] = value.astype(BF16)
+
+
+def finish(sc, off, dkv, tots, base):
+    width = dkv.shape[2]
+    shape = (2, 2, BLOCK, width)
     return pl.pallas_call(
         finish_kernel,
         grid_spec=pltpu.PrefetchScalarGridSpec(
             num_scalar_prefetch=2,
             grid=(width // HDIM,),
-            in_specs=[
-                pl.BlockSpec((OWN, HDIM), lambda h, sc, off: (0, h)),
-                pl.BlockSpec((2, OWN, HDIM), lambda h, sc, off: (0, 0, h)),
-            ]
-            + [pl.BlockSpec((2, BLOCK, HDIM), lambda h, sc, off: (0, 0, h))] * SIDE,
-            out_specs=[pl.BlockSpec((2, 3, BLOCK, HDIM), lambda h, sc, off: (0, 0, 0, h))] * SIDE,
+            in_specs=[pl.BlockSpec((2, OWN, HDIM), lambda h, sc, off: (0, 0, h))]
+            + [pl.BlockSpec((2, BLOCK, HDIM), lambda h, sc, off: (0, 0, base + h))] * SIDE,
+            out_specs=[pl.BlockSpec((2, 2, BLOCK, HDIM), lambda h, sc, off: (0, 0, 0, h))] * SIDE,
         ),
         out_shape=[jax.ShapeDtypeStruct(shape, BF16)] * SIDE,
         compiler_params=params(),
-        cost_estimate=cost(0, 20 * OWN * width),
+        cost_estimate=cost(0, 16 * OWN * width),
         name="finish",
-    )(sc, off, dq, dkv, *tots)
-
-
-def place_kernel(sc, off, *refs):
-    groups = len(SIZES)
-    outs = refs[(SIDE + 1) * groups :]
+    )(sc, off, dkv, *tots)
+
+
+def cut_kernel(sc, off, *refs):
+    core, x = sc[1], sc[4]
+    ins, outs = refs[: len(SIZES)], refs[len(SIZES) :]
+    for step in range(SIDE):
+        for side in range(2):
+            block = ((core + side) & 1) * SIDE + ((x + step) & 3)
+            rows = pl.ds(pl.multiple_of(block * BLOCK, BLOCK), BLOCK)
+            at = 0
+            for ref, heads in zip(ins, SIZES):
+                outs[step][side, 0, :, at : at + heads * HDIM] = ref[rows, :]
+                at += heads * HDIM
+
+
+def cut(sc, off, dqs):
+    shape = (2, 1, BLOCK, sum(SIZES) * HDIM)
+    return pl.pallas_call(
+        cut_kernel,
+        grid_spec=pltpu.PrefetchScalarGridSpec(
+            num_scalar_prefetch=2,
+            grid=(1,),
+            in_specs=[whole(dq.shape) for dq in dqs],
+            out_specs=[whole(shape)] * SIDE,
+        ),
+        out_shape=[jax.ShapeDtypeStruct(shape, BF16)] * SIDE,
+        compiler_params=params(),
+        cost_estimate=cost(0, 4 * OWN * shape[3]),
+        name="cut",
+    )(sc, off, *dqs)
+
+
+def place_kernel(sizes, sc, off, *refs):
+    outs = refs[(SIDE + 1) * len(sizes) :]
     x, core = sc[4], sc[1]
-    heads = sum(SIZES)
+    heads = sum(sizes)
     at = 0
-    for g in range(groups):
-        width = SIZES[g] * HDIM
+    for g, size in enumerate(sizes):
+        width = size * HDIM
         for step in range(SIDE):
             source = (x + SIDE - step) & 3
             for part in range(2):
                 side = core if part == 0 else 1 - core
                 first = pl.multiple_of(((source * 2 + side) * heads + at) * HDIM, HDIM)
                 ref = refs[g * (SIDE + 1) + (step if part == 0 else SIDE)]
-                for n in range(3):
-                    outs[n][:, pl.ds(first, width)] = ref[0 if part == 0 else step, n]
-        at += SIZES[g]
-
-
-def place(sc, off, parts):
-    columns = sum(SIZES) * HDIM * 2 * SIDE
+                for n, out in enumerate(outs):
+                    out[:, pl.ds(first, width)] = ref[0 if part == 0 else step, n]
+        at += size
+
+
+def place(sc, off, parts, count, sizes):
+    columns = sum(sizes) * HDIM * 2 * SIDE
     shape = (BLOCK, columns)
     specs = []
     for n, p in enumerate(parts):
         lead = SIDE if n % (SIDE + 1) == SIDE else 1
         specs.append(pl.BlockSpec((lead, *p.shape[1:]), lambda i, sc, off: (0, 0, 0, 0)))
     return pl.pallas_call(
-        place_kernel,
+        functools.partial(place_kernel, sizes),
         grid_spec=pltpu.PrefetchScalarGridSpec(
             num_scalar_prefetch=2,
             grid=(1,),
             in_specs=specs,
-            out_specs=[whole(shape)] * 3,
-        ),
-        out_shape=[jax.ShapeDtypeStruct(shape, BF16)] * 3,
-        compiler_params=params(),
-        cost_estimate=cost(0, 12 * BLOCK * columns),
+            out_specs=[whole(shape)] * count,
+        ),
+        out_shape=[jax.ShapeDtypeStruct(shape, BF16)] * count,
+        compiler_params=params(),
+        cost_estimate=cost(0, 4 * count * BLOCK * columns),
         name="place",
     )(sc, off, *parts)
+
+
+def spread_out(cuts):
+    there = [cuts[0]]
+    there += [named(cuts[n], along_x(n), "tp") for n in range(1, SIDE)]
+    return there + [named(jnp.concatenate([t[1:] for t in there], axis=0), SWAP)]
 
 
 def named(value, pairs, axis="ctx"):
@@ -562,24 +593,30 @@
         qd, kv = halo_of(sc, off, own, recv)
         work.append((own, recv, named(kv, ring(1)), named(qd, ring(-1))))
 
-    parts = []
-    for g, heads in enumerate(SIZES):
+    dqs, sents, dkvs, stats = [], [], [], []
+    for g in range(len(SIZES)):
         own, recv, kv, qd = work[g]
         dq, dkv, stat, sent = attn(sc, off, own, recv, kv, sums, bases[g])
-        stat = named(stat, ring(-1))
-        dkv = later(sc, off, own, recv, qd, stat, dkv)
-        part = sent[:, :BLOCK].astype(F32)
-        for n in range(1, NSUM):
-            moved = named(sent[:, n * BLOCK : (n + 1) * BLOCK], along_y(-n))
-            part = part + moved.astype(F32)
-        part = part.astype(BF16)
-        tots = [part] + [named(part, along_z(n)) for n in range(1, SIDE)]
-        cuts = finish(sc, off, dq, dkv, tots)
-        there = [cuts[0]]
-        there += [named(cuts[n], along_x(n), "tp") for n in range(1, SIDE)]
-        parts += there
-        parts.append(named(jnp.concatenate([t[1:] for t in there], axis=0), SWAP))
-    return tuple(place(sc, off, parts))
+        stats.append(named(stat, ring(-1)))
+        dqs.append(dq)
+        dkvs.append(dkv)
+        sents.append(sent)
+    sent = jnp.concatenate(sents, axis=2)
+    part = sent[:, :BLOCK].astype(F32)
+    for n in range(1, NSUM):
+        moved = named(sent[:, n * BLOCK : (n + 1) * BLOCK], along_y(-n))
+        part = part + moved.astype(F32)
+    part = part.astype(BF16)
+    tots = [part] + [named(part, along_z(n)) for n in range(1, SIDE)]
+    cuts = cut(sc, off, dqs)
+    grad_q = place(sc, off, spread_out(cuts), 1, (sum(SIZES),))
+    parts = []
+    for g in range(len(SIZES)):
+        own, recv, kv, qd = work[g]
+        dkv = later(sc, off, own, recv, qd, stats[g], dkvs[g])
+        cuts = finish(sc, off, dkv, tots, bases[g])
+        parts += spread_out(cuts)
+    return (*grad_q, *place(sc, off, parts, 2, SIZES))
 
 
 def solution(mesh):

time: 252 us -> 267 us (1.060)
  the two profiles are of different devices: /device:TPU:8 before, /device:TPU:1 now
where the time goes in v1:
time: 267 us; the launch traced here: 266 us
  waiting for transfers between devices  105 us (39%)
  Pallas kernels  101 us (38%)
  starting transfers between devices  44.2 us (17%)
  local copies, waits for them, and re-layouts  12.2 us (5%)
    ppermute x36, waiting for transfers between devices, named(): return lax.ppermute(value, axis, pairs)  105 us
    ppermute x36, starting transfers between devices, named(): return lax.ppermute(value, axis, pairs)  44.2 us
    pallas_call x2, Pallas kernels, attn(): pl.pallas_call(attn_kernel, grid_spec=pltpu.PrefetchScalarGridSpec(num_sc...  37.7 us
    pallas_call x2, Pallas kernels, later(): pl.pallas_call(later_kernel, grid_spec=pltpu.PrefetchScalarGridSpec(num_s...  15.8 us
    unnamed x81, local copies, waits for them, and re-layouts  11.2 us
    pallas_call x2, Pallas kernels, halo_of(): pl.pallas_call(halo_kernel, grid_spec=pltpu.PrefetchScalarGridSpec(num_sc...  10.4 us
    pallas_call x2, Pallas kernels, finish(): pl.pallas_call(finish_kernel, grid_spec=pltpu.PrefetchScalarGridSpec(num_...  9.46 us
    pallas_call x2, Pallas kernels, pack(): pl.pallas_call(pack_kernel, grid_spec=pltpu.PrefetchScalarGridSpec(num_sc...  8.02 us
  transfers between devices with their start and end apart: 36, of which 14 were waited for; matrix products, arithmetic and copies ran while one was open for 1% of the time, Pallas kernels for 35%

profile of v1, /device:TPU:1, one launch (start us, length us, event | category | flops | bytes accessed | tf_op | source)
XLA Modules:
  0.0 265.7 jit_solution(16531522715754312699)
XLA Ops:
  1.1 4.0 %pack.3 = (bf16[4,512,384]{2,1,0:T(8,128)(2,1)}, bf16[4,512,384]{2,1,0:T(8,128)(2,1)}) custom-call(s32[8]{0:T(128)} %compare_select_fusion.3.sc, s32[4]{0:T(128)} %off.31, bf16[512,1536]{1,0:T(8,128)(2,1)} %refs_1_.3, bf16[512,1536]{1,0:T(8,128)(2,1)} %refs_1_.3, bf16[512,1536]{1,0:T(8,128)(2,1)} %refs_3_.3, bf16[512,1536]{1,0:T(8,128)(2,1)} %refs_3_.3, ...), custom_call_target="tpu_custom_call" | custom-call | bytes 6291456 | tf_op jit(solution)/shard_map/pack/pallas_call | solution.py:102
  6.5 4.0 %pack.2 = (bf16[4,512,384]{2,1,0:T(8,128)(2,1)}, bf16[4,512,384]{2,1,0:T(8,128)(2,1)}) custom-call(s32[8]{0:T(128)} %compare_select_fusion.3.sc, s32[4]{0:T(128)} %off.31, bf16[512,1536]{1,0:T(8,128)(2,1)} %refs_1_.3, bf16[512,1536]{1,0:T(8,128)(2,1)} %refs_1_.3, bf16[512,1536]{1,0:T(8,128)(2,1)} %refs_3_.3, bf16[512,1536]{1,0:T(8,128)(2,1)} %refs_3_.3, ...), custom_call_target="tpu_custom_call" | custom-call | bytes 6291456 | tf_op jit(solution)/shard_map/pack/pallas_call | solution.py:102
  11.7 5.1 %halo.3 = (bf16[2,896,384]{2,1,0:T(8,128)(2,1)}, bf16[2,896,384]{2,1,0:T(8,128)(2,1)}) custom-call(s32[8]{0:T(128)} %compare_select_fusion.3.sc, s32[4]{0:T(128)} %off.31, bf16[4,512,384]{2,1,0:T(8,128)(2,1)} %get-tuple-element.49.own, bf16[4,512,384]{2,1,0:T(8,128)(2,1)} %copy-done.1), custom_call_target="tpu_custom_call" | custom-call | bytes 12582912 | tf_op jit(solution)/shard_map/halo/pallas_call | solution.py:138
  32.3 22.5 %collective-permute-done.4 = bf16[2,32,768]{2,1,0:T(8,128)(2,1)S(1)} collective-permute-done((bf16[2,32,768]{2,1,0:T(8,128)(2,1)}, bf16[2,32,768]{2,1,0:T(8,128)(2,1)S(1)}, u32[]{:S(2)}, u32[]{:S(2)}) %collective-permute-start.4) | collective-permute-done | bytes 98336 | tf_op jit(solution)/shard_map/ppermute | solution.py:562
  61.8 5.0 %collective-permute-done.6.refs_1_ = bf16[2,32,768]{2,1,0:T(8,128)(2,1)S(1)} collective-permute-done((bf16[2,32,768]{2,1,0:T(8,128)(2,1)S(1)}, bf16[2,32,768]{2,1,0:T(8,128)(2,1)S(1)}, u32[]{:S(2)}, u32[]{:S(2)}) %collective-permute-start.6) | collective-permute-done | bytes 98336 | tf_op jit(solution)/shard_map/ppermute | solution.py:562
  73.3 5.3 %halo.2 = (bf16[2,896,384]{2,1,0:T(8,128)(2,1)}, bf16[2,896,384]{2,1,0:T(8,128)(2,1)}) custom-call(s32[8]{0:T(128)} %compare_select_fusion.3.sc, s32[4]{0:T(128)} %off.31, bf16[4,512,384]{2,1,0:T(8,128)(2,1)} %get-tuple-element.39.own, bf16[4,512,384]{2,1,0:T(8,128)(2,1)} %copy-done), custom_call_target="tpu_custom_call" | custom-call | bytes 12582912 | tf_op jit(solution)/shard_map/halo/pallas_call | solution.py:138
  78.5 3.6 %collective-permute-done.10.s2 = bf16[2,128,768]{2,1,0:T(8,128)(2,1)S(1)} collective-permute-done((bf16[2,128,768]{2,1,0:T(8,128)(2,1)}, bf16[2,128,768]{2,1,0:T(8,128)(2,1)S(1)}, u32[]{:S(2)}, u32[]{:S(2)}) %collective-permute-start.10) | collective-permute-done | bytes 393248 | tf_op jit(solution)/shard_map/ppermute | solution.py:562
  83.4 3.8 %collective-permute-done.11.s3 = bf16[2,128,768]{2,1,0:T(8,128)(2,1)S(1)} collective-permute-done((bf16[2,128,768]{2,1,0:T(8,128)(2,1)}, bf16[2,128,768]{2,1,0:T(8,128)(2,1)S(1)}, u32[]{:S(2)}, u32[]{:S(2)}) %collective-permute-start.11) | collective-permute-done | bytes 393248 | tf_op jit(solution)/shard_map/ppermute | solution.py:562
  87.2 5.8 %collective-permute-start.18 = (bf16[2,896,384]{2,1,0:T(8,128)(2,1)}, bf16[2,896,384]{2,1,0:T(8,128)(2,1)S(1)}, u32[]{:S(2)}, u32[]{:S(2)}) collective-permute-start(bf16[2,896,384]{2,1,0:T(8,128)(2,1)} %get-tuple-element.57), channel_id=1, source_target_pairs={{0,120},{4,124},{8,0},{12,4},{16,8},{20,12},{24,16},{28,20},{32,24... | collective-permute-start | bytes 4128776 | tf_op jit(solution)/shard_map/ppermute | solution.py:562
  93.0 18.9 %attn.3 = (bf16[1024,384]{1,0:T(8,128)(2,1)}, f32[2,1024,384]{2,1,0:T(8,128)}, f32[3,8,1024]{2,1,0:T(8,128)}, bf16[2,512,384]{2,1,0:T(8,128)(2,1)}) custom-call(s32[8]{0:T(128)} %compare_select_fusion.3.sc, s32[4]{0:T(128)} %off.31, bf16[4,512,384]{2,1,0:T(8,128)(2,1)} %get-tuple-element.49.own, bf16[4,512,384]{2,1,0:T(8,128)(2,1)} %copy-done.1, ...), custom_call_target="tpu_custom_call" | custom-call | flops 12079595520 | bytes 12000000 | tf_op jit(solution)/shard_map/attn/pallas_call | solution.py:413
  111.9 11.2 %collective-permute-done.1.halo = bf16[2,896,384]{2,1,0:T(8,128)(2,1)S(1)} collective-permute-done((bf16[2,896,384]{2,1,0:T(8,128)(2,1)}, bf16[2,896,384]{2,1,0:T(8,128)(2,1)S(1)}, u32[]{:S(2)}, u32[]{:S(2)}) %collective-permute-start.1) | collective-permute-done | bytes 1376288 | tf_op jit(solution)/shard_map/ppermute | solution.py:562
  124.3 18.8 %attn.2 = (bf16[1024,384]{1,0:T(8,128)(2,1)}, f32[2,1024,384]{2,1,0:T(8,128)}, f32[3,8,1024]{2,1,0:T(8,128)}, bf16[2,512,384]{2,1,0:T(8,128)(2,1)}) custom-call(s32[8]{0:T(128)} %compare_select_fusion.3.sc, s32[4]{0:T(128)} %off.31, bf16[4,512,384]{2,1,0:T(8,128)(2,1)} %get-tuple-element.39.own, bf16[4,512,384]{2,1,0:T(8,128)(2,1)} %copy-done, ...), custom_call_target="tpu_custom_call" | custom-call | flops 12079595520 | bytes 12000000 | tf_op jit(solution)/shard_map/attn/pallas_call | solution.py:413
  146.3 8.7 %collective-permute-done.20 = bf16[2,128,768]{2,1,0:T(8,128)(2,1)S(1)} collective-permute-done((bf16[2,128,768]{2,1,0:T(8,128)(2,1)S(1)}, bf16[2,128,768]{2,1,0:T(8,128)(2,1)S(1)}, u32[]{:S(2)}, u32[]{:S(2)}) %collective-permute-start.20) | collective-permute-done | bytes 393248 | tf_op jit(solution)/shard_map/ppermute | solution.py:562
  156.1 9.7 %collective-permute-done.22 = bf16[2,128,768]{2,1,0:T(8,128)(2,1)S(1)} collective-permute-done((bf16[2,128,768]{2,1,0:T(8,128)(2,1)S(1)}, bf16[2,128,768]{2,1,0:T(8,128)(2,1)S(1)}, u32[]{:S(2)}, u32[]{:S(2)}) %collective-permute-start.22) | collective-permute-done | bytes 393248 | tf_op jit(solution)/shard_map/ppermute | solution.py:562
  172.6 18.0 %collective-permute-done.31.stat = f32[3,8,1024]{2,1,0:T(8,128)S(1)} collective-permute-done((f32[3,8,1024]{2,1,0:T(8,128)S(1)}, f32[3,8,1024]{2,1,0:T(8,128)S(1)}, u32[]{:S(2)}, u32[]{:S(2)}) %collective-permute-start.31) | collective-permute-done | bytes 98336 | tf_op jit(solution)/shard_map/ppermute | solution.py:562
  191.8 8.0 %later.3.dkv = f32[2,1024,384]{2,1,0:T(8,128)} custom-call(s32[8]{0:T(128)} %compare_select_fusion.3.sc, s32[4]{0:T(128)} %off.31, bf16[4,512,384]{2,1,0:T(8,128)(2,1)} %get-tuple-element.49.own, bf16[4,512,384]{2,1,0:T(8,128)(2,1)} %copy-done.1, bf16[2,896,384]{2,1,0:T(8,128)(2,1)} %copy-done.7, f32[3,8,1024]{2,1,0:T(8,128)} %copy-done.28, ...), custom_call_target="tpu_custom_call" | custom-call | flops 2818572288 | bytes 12000000 | tf_op jit(solution)/shard_map/later/pallas_call | solution.py:382
  204.3 4.7 %finish.3 = (bf16[2,2,128,384]{3,2,1,0:T(8,128)(2,1)}, bf16[2,2,128,384]{3,2,1,0:T(8,128)(2,1)}, bf16[2,2,128,384]{3,2,1,0:T(8,128)(2,1)}, bf16[2,2,128,384]{3,2,1,0:T(8,128)(2,1)}) custom-call(s32[8]{0:T(128)} %compare_select_fusion.3.sc, s32[4]{0:T(128)} %off.31, f32[2,1024,384]{2,1,0:T(8,128)} %later.3.dkv, bf16[2,128,768]{2,1,0:T(8,128)(2,1)} %copy-done.2, ...), custom_call_target="tpu_custom_call" | custom-call | bytes 6291456 | tf_op jit(solution)/shard_map/finish/pallas_call | solution.py:469
  209.4 3.5 %collective-permute-done.19.stat = f32[3,8,1024]{2,1,0:T(8,128)S(1)} collective-permute-done((f32[3,8,1024]{2,1,0:T(8,128)S(1)}, f32[3,8,1024]{2,1,0:T(8,128)S(1)}, u32[]{:S(2)}, u32[]{:S(2)}) %collective-permute-start.19) | collective-permute-done | bytes 98336 | tf_op jit(solution)/shard_map/ppermute | solution.py:562
  215.6 7.8 %later.2.dkv = f32[2,1024,384]{2,1,0:T(8,128)} custom-call(s32[8]{0:T(128)} %compare_select_fusion.3.sc, s32[4]{0:T(128)} %off.31, bf16[4,512,384]{2,1,0:T(8,128)(2,1)} %get-tuple-element.39.own, bf16[4,512,384]{2,1,0:T(8,128)(2,1)} %copy-done, bf16[2,896,384]{2,1,0:T(8,128)(2,1)} %copy-done.6, f32[3,8,1024]{2,1,0:T(8,128)} %copy-done.27, ...), custom_call_target="tpu_custom_call" | custom-call | flops 2818572288 | bytes 12000000 | tf_op jit(solution)/shard_map/later/pallas_call | solution.py:382
  223.4 4.8 %finish.2 = (bf16[2,2,128,384]{3,2,1,0:T(8,128)(2,1)}, bf16[2,2,128,384]{3,2,1,0:T(8,128)(2,1)}, bf16[2,2,128,384]{3,2,1,0:T(8,128)(2,1)}, bf16[2,2,128,384]{3,2,1,0:T(8,128)(2,1)}) custom-call(s32[8]{0:T(128)} %compare_select_fusion.3.sc, s32[4]{0:T(128)} %off.31, f32[2,1024,384]{2,1,0:T(8,128)} %later.2.dkv, bf16[2,128,768]{2,1,0:T(8,128)(2,1)} %copy-done.2, ...), custom_call_target="tpu_custom_call" | custom-call | bytes 6291456 | tf_op jit(solution)/shard_map/finish/pallas_call | solution.py:469
  233.9 5.0 %collective-permute-start.17 = (bf16[4,1,128,768]{3,2,1,0:T(8,128)(2,1)S(1)}, bf16[4,1,128,768]{3,2,1,0:T(8,128)(2,1)S(1)}, u32[]{:S(2)}, u32[]{:S(2)}) collective-permute-start(bf16[4,1,128,768]{3,2,1,0:T(8,128)(2,1)S(1)} %pad_maximum_fusion), channel_id=1, source_target_pairs={{0,4},{4,0},{8,12},{12,8},{16,20},{20,16},{24,28},{28,24},{32,36},... | collective-permute-start | bytes 2359304 | tf_op jit(solution)/shard_map/ppermute | solution.py:562
  240.1 4.2 %collective-permute-done.27.refs_2_ = bf16[2,2,128,384]{3,2,1,0:T(8,128)(2,1)S(1)} collective-permute-done((bf16[2,2,128,384]{3,2,1,0:T(8,128)(2,1)}, bf16[2,2,128,384]{3,2,1,0:T(8,128)(2,1)S(1)}, u32[]{:S(2)}, u32[]{:S(2)}) %collective-permute-start.27) | collective-permute-done | bytes 393248 | tf_op jit(solution)/shard_map/ppermute | solution.py:562
  244.3 8.8 %collective-permute-done.28.refs_3_ = bf16[2,2,128,384]{3,2,1,0:T(8,128)(2,1)S(1)} collective-permute-done((bf16[2,2,128,384]{3,2,1,0:T(8,128)(2,1)}, bf16[2,2,128,384]{3,2,1,0:T(8,128)(2,1)S(1)}, u32[]{:S(2)}, u32[]{:S(2)}) %collective-permute-start.28) | collective-permute-done | bytes 393248 | tf_op jit(solution)/shard_map/ppermute | solution.py:562
  261.1 4.6 %place.3 = (bf16[128,6144]{1,0:T(8,128)(2,1)}, bf16[128,6144]{1,0:T(8,128)(2,1)}) custom-call(s32[8]{0:T(128)} %compare_select_fusion.3.sc, s32[4]{0:T(128)} %off.31, bf16[2,2,128,384]{3,2,1,0:T(8,128)(2,1)} %get-tuple-element.62.refs_0_, bf16[2,2,128,384]{3,2,1,0:T(8,128)(2,1)} %copy-done.17, bf16[2,2,128,384]{3,2,1,0:T(8,128)(2,1)} %copy-done.18, ...), custom_call_target="tpu_custom_call" | custom-call | bytes 6291456 | tf_op jit(solution)/shard_map/place/pallas_call | solution.py:540
  (166 shorter events, 68.2 us)
Async XLA Ops:
  10.5 61.6 %collective-permute-start = (bf16[4,512,384]{2,1,0:T(8,128)(2,1)}, bf16[4,512,384]{2,1,0:T(8,128)(2,1)S(1)}, u32[]{:S(2)}, u32[]{:S(2)}) collective-permute-start(bf16[4,512,384]{2,1,0:T(8,128)(2,1)} %get-tuple-element.40), channel_id=1, source_target_pairs={{0,4},{4,0},{8,12},{12,8},{16,20},{20,16},{24,28},{28,24},{32,36},... | collective-permute-start | bytes 4718600 | tf_op jit(solution)/shard_map/ppermute | solution.py:562
  16.8 76.2 %collective-permute-start.13 = (bf16[2,896,384]{2,1,0:T(8,128)(2,1)}, bf16[2,896,384]{2,1,0:T(8,128)(2,1)}, u32[]{:S(2)}, u32[]{:S(2)}) collective-permute-start(bf16[2,896,384]{2,1,0:T(8,128)(2,1)} %get-tuple-element.51), channel_id=1, source_target_pairs={{0,8},{4,12},{8,16},{12,20},{16,24},{20,28},{24,32},{28,36},{32,40... | collective-permute-start | bytes 4128776 | tf_op jit(solution)/shard_map/ppermute | solution.py:562
  29.0 25.8 %collective-permute-start.4 = (bf16[2,32,768]{2,1,0:T(8,128)(2,1)}, bf16[2,32,768]{2,1,0:T(8,128)(2,1)S(1)}, u32[]{:S(2)}, u32[]{:S(2)}) collective-permute-start(bf16[2,32,768]{2,1,0:T(8,128)(2,1)} %get-tuple-element.45), channel_id=1, source_target_pairs={{0,16},{4,20},{8,24},{12,28},{16,0},{20,4},{24,8},{28,12},{32,48},... | collective-permute-start | bytes 294920 | tf_op jit(solution)/shard_map/ppermute | solution.py:562
  30.4 27.8 %collective-permute-start.5 = (bf16[2,32,768]{2,1,0:T(8,128)(2,1)}, bf16[2,32,768]{2,1,0:T(8,128)(2,1)S(1)}, u32[]{:S(2)}, u32[]{:S(2)}) collective-permute-start(bf16[2,32,768]{2,1,0:T(8,128)(2,1)} %get-tuple-element.46), channel_id=1, source_target_pairs={{0,8},{4,12},{8,16},{12,20},{16,24},{20,28},{24,0},{28,4},{32,40},... | collective-permute-start | bytes 294920 | tf_op jit(solution)/shard_map/ppermute | solution.py:562
  70.6 16.6 %collective-permute-start.11 = (bf16[2,128,768]{2,1,0:T(8,128)(2,1)}, bf16[2,128,768]{2,1,0:T(8,128)(2,1)S(1)}, u32[]{:S(2)}, u32[]{:S(2)}) collective-permute-start(bf16[2,128,768]{2,1,0:T(8,128)(2,1)} %gather.1.s0), channel_id=1, source_target_pairs={{0,96},{4,100},{8,104},{12,108},{16,112},{20,116},{24,120},{28,124... | collective-permute-start | bytes 1179656 | tf_op jit(solution)/shard_map/ppermute | solution.py:562
  70.6 22.4 %collective-permute-start.9 = (bf16[2,128,768]{2,1,0:T(8,128)(2,1)}, bf16[2,128,768]{2,1,0:T(8,128)(2,1)}, u32[]{:S(2)}, u32[]{:S(2)}) collective-permute-start(bf16[2,128,768]{2,1,0:T(8,128)(2,1)} %gather.1.s0), channel_id=1, source_target_pairs={{0,32},{4,36},{8,40},{12,44},{16,48},{20,52},{24,56},{28,60},{32,6... | collective-permute-start | bytes 1179656 | tf_op jit(solution)/shard_map/ppermute | solution.py:562
  78.5 44.6 %collective-permute-start.1 = (bf16[2,896,384]{2,1,0:T(8,128)(2,1)}, bf16[2,896,384]{2,1,0:T(8,128)(2,1)S(1)}, u32[]{:S(2)}, u32[]{:S(2)}) collective-permute-start(bf16[2,896,384]{2,1,0:T(8,128)(2,1)} %get-tuple-element.41), channel_id=1, source_target_pairs={{0,8},{4,12},{8,16},{12,20},{16,24},{20,28},{24,32},{28,36},{32,40... | collective-permute-start | bytes 4128776 | tf_op jit(solution)/shard_map/ppermute | solution.py:562
  82.2 86.6 %collective-permute-start.30 = (bf16[2,896,384]{2,1,0:T(8,128)(2,1)S(1)}, bf16[2,896,384]{2,1,0:T(8,128)(2,1)S(1)}, u32[]{:S(2)}, u32[]{:S(2)}) collective-permute-start(bf16[2,896,384]{2,1,0:T(8,128)(2,1)S(1)} %copy-done.32), channel_id=1, source_target_pairs={{0,120},{4,124},{8,0},{12,4},{16,8},{20,12},{24,16},{28,20},{32,24... | collective-permute-start | bytes 4128776 | tf_op jit(solution)/shard_map/ppermute | solution.py:562
  87.2 122.1 %collective-permute-start.18 = (bf16[2,896,384]{2,1,0:T(8,128)(2,1)}, bf16[2,896,384]{2,1,0:T(8,128)(2,1)S(1)}, u32[]{:S(2)}, u32[]{:S(2)}) collective-permute-start(bf16[2,896,384]{2,1,0:T(8,128)(2,1)} %get-tuple-element.57), channel_id=1, source_target_pairs={{0,120},{4,124},{8,0},{12,4},{16,8},{20,12},{24,16},{28,20},{32,24... | collective-permute-start | bytes 4128776 | tf_op jit(solution)/shard_map/ppermute | solution.py:562
  144.9 21.0 %collective-permute-start.22 = (bf16[2,128,768]{2,1,0:T(8,128)(2,1)S(1)}, bf16[2,128,768]{2,1,0:T(8,128)(2,1)S(1)}, u32[]{:S(2)}, u32[]{:S(2)}) collective-permute-start(bf16[2,128,768]{2,1,0:T(8,128)(2,1)S(1)} %get-tuple-element.76), channel_id=1, source_target_pairs={{0,32},{4,36},{8,40},{12,44},{16,48},{20,52},{24,56},{28,60},{32,6... | collective-permute-start | bytes 1179656 | tf_op jit(solution)/shard_map/ppermute | solution.py:562
  166.1 33.7 %collective-permute-start.23 = (bf16[2,128,768]{2,1,0:T(8,128)(2,1)S(1)}, bf16[2,128,768]{2,1,0:T(8,128)(2,1)S(1)}, u32[]{:S(2)}, u32[]{:S(2)}) collective-permute-start(bf16[2,128,768]{2,1,0:T(8,128)(2,1)S(1)} %add_convert_fusion.refs_0_), channel_id=1, source_target_pairs={{0,8},{4,12},{8,16},{12,20},{16,24},{20,28},{24,0},{28,4},{32,40},... | collective-permute-start | bytes 1179656 | tf_op jit(solution)/shard_map/ppermute | solution.py:562
  166.2 36.2 %collective-permute-start.24 = (bf16[2,128,768]{2,1,0:T(8,128)(2,1)S(1)}, bf16[2,128,768]{2,1,0:T(8,128)(2,1)S(1)}, u32[]{:S(2)}, u32[]{:S(2)}) collective-permute-start(bf16[2,128,768]{2,1,0:T(8,128)(2,1)S(1)} %add_convert_fusion.refs_0_), channel_id=1, source_target_pairs={{0,16},{4,20},{8,24},{12,28},{16,0},{20,4},{24,8},{28,12},{32,48},... | collective-permute-start | bytes 1179656 | tf_op jit(solution)/shard_map/ppermute | solution.py:562
  166.3 37.3 %collective-permute-start.25 = (bf16[2,128,768]{2,1,0:T(8,128)(2,1)S(1)}, bf16[2,128,768]{2,1,0:T(8,128)(2,1)S(1)}, u32[]{:S(2)}, u32[]{:S(2)}) collective-permute-start(bf16[2,128,768]{2,1,0:T(8,128)(2,1)S(1)} %add_convert_fusion.refs_0_), channel_id=1, source_target_pairs={{0,24},{4,28},{8,0},{12,4},{16,8},{20,12},{24,16},{28,20},{32,56},... | collective-permute-start | bytes 1179656 | tf_op jit(solution)/shard_map/ppermute | solution.py:562
  168.8 21.7 %collective-permute-start.31 = (f32[3,8,1024]{2,1,0:T(8,128)S(1)}, f32[3,8,1024]{2,1,0:T(8,128)S(1)}, u32[]{:S(2)}, u32[]{:S(2)}) collective-permute-start(f32[3,8,1024]{2,1,0:T(8,128)S(1)} %copy-done.39), channel_id=1, source_target_pairs={{0,120},{4,124},{8,0},{12,4},{16,8},{20,12},{24,16},{28,20},{32,24... | collective-permute-start | bytes 294920 | tf_op jit(solution)/shard_map/ppermute | solution.py:562
  190.6 24.1 %collective-permute-start.14 = (bf16[2,1,128,768]{3,2,1,0:T(8,128)(2,1)}, bf16[2,1,128,768]{3,2,1,0:T(8,128)(2,1)S(1)}, u32[]{:S(2)}, u32[]{:S(2)}) collective-permute-start(bf16[2,1,128,768]{3,2,1,0:T(8,128)(2,1)} %get-tuple-element.54), channel_id=1, source_target_pairs={{0,1},{1,2},{2,3},{3,0},{4,5},{5,6},{6,7},{7,4},{8,9},{9,10},{10,1... | collective-permute-start | bytes 1179656 | tf_op jit(solution)/shard_map/ppermute | solution.py:562
  199.8 28.4 %collective-permute-start.15 = (bf16[2,1,128,768]{3,2,1,0:T(8,128)(2,1)S(1)}, bf16[2,1,128,768]{3,2,1,0:T(8,128)(2,1)S(1)}, u32[]{:S(2)}, u32[]{:S(2)}) collective-permute-start(bf16[2,1,128,768]{3,2,1,0:T(8,128)(2,1)S(1)} %copy-done.35), channel_id=1, source_target_pairs={{0,2},{1,3},{2,0},{3,1},{4,6},{5,7},{6,4},{7,5},{8,10},{9,11},{10,... | collective-permute-start | bytes 1179656 | tf_op jit(solution)/shard_map/ppermute | solution.py:562
  202.4 26.5 %collective-permute-start.16 = (bf16[2,1,128,768]{3,2,1,0:T(8,128)(2,1)S(1)}, bf16[2,1,128,768]{3,2,1,0:T(8,128)(2,1)S(1)}, u32[]{:S(2)}, u32[]{:S(2)}) collective-permute-start(bf16[2,1,128,768]{3,2,1,0:T(8,128)(2,1)S(1)} %copy-done.34), channel_id=1, source_target_pairs={{0,3},{1,0},{2,1},{3,2},{4,7},{5,4},{6,5},{7,6},{8,11},{9,8},{10,9... | collective-permute-start | bytes 1179656 | tf_op jit(solution)/shard_map/ppermute | solution.py:562
  209.0 21.7 %collective-permute-start.32 = (bf16[2,2,128,384]{3,2,1,0:T(8,128)(2,1)}, bf16[2,2,128,384]{3,2,1,0:T(8,128)(2,1)S(1)}, u32[]{:S(2)}, u32[]{:S(2)}) collective-permute-start(bf16[2,2,128,384]{3,2,1,0:T(8,128)(2,1)} %get-tuple-element.70), channel_id=1, source_target_pairs={{0,1},{1,2},{2,3},{3,0},{4,5},{5,6},{6,7},{7,4},{8,9},{9,10},{10,1... | collective-permute-start | bytes 1179656 | tf_op jit(solution)/shard_map/ppermute | solution.py:562
  212.9 21.0 %collective-permute-start.33 = (bf16[2,2,128,384]{3,2,1,0:T(8,128)(2,1)}, bf16[2,2,128,384]{3,2,1,0:T(8,128)(2,1)S(1)}, u32[]{:S(2)}, u32[]{:S(2)}) collective-permute-start(bf16[2,2,128,384]{3,2,1,0:T(8,128)(2,1)} %get-tuple-element.71), channel_id=1, source_target_pairs={{0,2},{1,3},{2,0},{3,1},{4,6},{5,7},{6,4},{7,5},{8,10},{9,11},{10,... | collective-permute-start | bytes 1179656 | tf_op jit(solution)/shard_map/ppermute | solution.py:562
  214.7 24.2 %collective-permute-start.34 = (bf16[2,2,128,384]{3,2,1,0:T(8,128)(2,1)}, bf16[2,2,128,384]{3,2,1,0:T(8,128)(2,1)S(1)}, u32[]{:S(2)}, u32[]{:S(2)}) collective-permute-start(bf16[2,2,128,384]{3,2,1,0:T(8,128)(2,1)} %get-tuple-element.72), channel_id=1, source_target_pairs={{0,3},{1,0},{2,1},{3,2},{4,7},{5,4},{6,5},{7,6},{8,11},{9,8},{10,9... | collective-permute-start | bytes 1179656 | tf_op jit(solution)/shard_map/ppermute | solution.py:562
  228.9 15.4 %collective-permute-start.27 = (bf16[2,2,128,384]{3,2,1,0:T(8,128)(2,1)}, bf16[2,2,128,384]{3,2,1,0:T(8,128)(2,1)S(1)}, u32[]{:S(2)}, u32[]{:S(2)}) collective-permute-start(bf16[2,2,128,384]{3,2,1,0:T(8,128)(2,1)} %get-tuple-element.64), channel_id=1, source_target_pairs={{0,2},{1,3},{2,0},{3,1},{4,6},{5,7},{6,4},{7,5},{8,10},{9,11},{10,... | collective-permute-start | bytes 1179656 | tf_op jit(solution)/shard_map/ppermute | solution.py:562
  230.7 22.4 %collective-permute-start.28 = (bf16[2,2,128,384]{3,2,1,0:T(8,128)(2,1)}, bf16[2,2,128,384]{3,2,1,0:T(8,128)(2,1)S(1)}, u32[]{:S(2)}, u32[]{:S(2)}) collective-permute-start(bf16[2,2,128,384]{3,2,1,0:T(8,128)(2,1)} %get-tuple-element.65), channel_id=1, source_target_pairs={{0,3},{1,0},{2,1},{3,2},{4,7},{5,4},{6,5},{7,6},{8,11},{9,8},{10,9... | collective-permute-start | bytes 1179656 | tf_op jit(solution)/shard_map/ppermute | solution.py:562
  233.9 21.1 %collective-permute-start.17 = (bf16[4,1,128,768]{3,2,1,0:T(8,128)(2,1)S(1)}, bf16[4,1,128,768]{3,2,1,0:T(8,128)(2,1)S(1)}, u32[]{:S(2)}, u32[]{:S(2)}) collective-permute-start(bf16[4,1,128,768]{3,2,1,0:T(8,128)(2,1)S(1)} %pad_maximum_fusion), channel_id=1, source_target_pairs={{0,4},{4,0},{8,12},{12,8},{16,20},{20,16},{24,28},{28,24},{32,36},... | collective-permute-start | bytes 2359304 | tf_op jit(solution)/shard_map/ppermute | solution.py:562
  239.1 20.1 %collective-permute-start.35 = (bf16[4,2,128,384]{3,2,1,0:T(8,128)(2,1)S(1)}, bf16[4,2,128,384]{3,2,1,0:T(8,128)(2,1)S(1)}, u32[]{:S(2)}, u32[]{:S(2)}) collective-permute-start(bf16[4,2,128,384]{3,2,1,0:T(8,128)(2,1)S(1)} %pad_maximum_fusion.2), channel_id=1, source_target_pairs={{0,4},{4,0},{8,12},{12,8},{16,20},{20,16},{24,28},{28,24},{32,36},... | collective-permute-start | bytes 2359304 | tf_op jit(solution)/shard_map/ppermute | solution.py:562
  (52 other events, 385.6 us)

commit v2 on v0

--- a/solution.py
+++ b/solution.py
@@ -401,7 +401,7 @@
     )(sc, off, own, recv, qd, stat, dkv)
 
 
-def attn(sc, off, own, recv, halo, sums, base):
+def attn(sc, off, own, recv, halo, sums):
     width = own.shape[2]
     heads = width // HDIM
     keys = EXT + NSUM * BLOCK
@@ -409,7 +409,7 @@
     def by_head(n, rows):
         return pl.BlockSpec((n, rows, HDIM), lambda h, sc, off: (0, 0, h))
 
-    sum_spec = pl.BlockSpec((2, BLOCK, HDIM), lambda h, sc, off: (0, 0, base + h))
+    sum_spec = pl.BlockSpec((2, BLOCK, HDIM), lambda h, sc, off: (0, 0, h))
     return pl.pallas_call(
         attn_kernel,
         grid_spec=pltpu.PrefetchScalarGridSpec(
@@ -552,7 +552,6 @@
         piece = jnp.where(step == n, arrived[n], piece)
     parts = [piece] + [named(piece, along_z(n)) for n in range(1, SIDE)]
     summary = gather(sc, off, parts)
-    sums = [summary] + [named(summary, along_y(n)) for n in range(1, NSUM)]
 
     bases = [sum(SIZES[:g]) for g in range(len(SIZES))]
     work = []
@@ -565,7 +564,9 @@
     parts = []
     for g, heads in enumerate(SIZES):
         own, recv, kv, qd = work[g]
-        dq, dkv, stat, sent = attn(sc, off, own, recv, kv, sums, bases[g])
+        mine = summary[:, :, bases[g] * HDIM : (bases[g] + heads) * HDIM]
+        sums = [mine] + [named(mine, along_y(n)) for n in range(1, NSUM)]
+        dq, dkv, stat, sent = attn(sc, off, own, recv, kv, sums)
         stat = named(stat, ring(-1))
         dkv = later(sc, off, own, recv, qd, stat, dkv)
         part = sent[:, :BLOCK].astype(F32)

time: 252 us -> 256 us (1.016)
  waiting for transfers between devices: 93.6 us -> 88 us
  starting transfers between devices: 44.9 us -> 50.4 us
    ppermute x38 -> x41, waiting for transfers between devices: 93.6 us -> 88 us  [named(): return lax.ppermute(value, axis, pairs)]
    ppermute x38 -> x41, starting transfers between devices: 44.9 us -> 50.4 us  [named(): return lax.ppermute(value, axis, pairs)]
    unnamed x72 -> x84, local copies, waits for them, and re-layouts: 7 us -> 7.74 us
  transfers between devices with their start and end apart: 38 -> 41, of which waited for: 16 -> 14; matrix products, arithmetic and copies ran while one was open for 2% -> 3% of each run, Pallas kernels for 35% -> 34%
where the time goes in v2:
time: 256 us; the launch traced here: 250 us
  Pallas kernels  95.5 us (37%)
  waiting for transfers between devices  88 us (34%)
  starting transfers between devices  50.4 us (20%)
  local copies, waits for them, and re-layouts  11.8 us (5%)
  other arithmetic  3 us (1%)
    ppermute x41, waiting for transfers between devices, named(): return lax.ppermute(value, axis, pairs)  88 us
    ppermute x41, starting transfers between devices, named(): return lax.ppermute(value, axis, pairs)  50.4 us
    pallas_call x2, Pallas kernels, attn(): pl.pallas_call(attn_kernel, grid_spec=pltpu.PrefetchScalarGridSpec(num_sc...  37.7 us
    pallas_call x2, Pallas kernels, later(): pl.pallas_call(later_kernel, grid_spec=pltpu.PrefetchScalarGridSpec(num_s...  15.7 us
    pallas_call x2, Pallas kernels, halo_of(): pl.pallas_call(halo_kernel, grid_spec=pltpu.PrefetchScalarGridSpec(num_sc...  10.3 us
    pallas_call x2, Pallas kernels, finish(): pl.pallas_call(finish_kernel, grid_spec=pltpu.PrefetchScalarGridSpec(num_...  10.3 us
    pallas_call x2, Pallas kernels, pack(): pl.pallas_call(pack_kernel, grid_spec=pltpu.PrefetchScalarGridSpec(num_sc...  8.04 us
    unnamed x84, local copies, waits for them, and re-layouts  7.74 us
  transfers between devices with their start and end apart: 41, of which 14 were waited for; matrix products, arithmetic and copies ran while one was open for 3% of the time, Pallas kernels for 34%

profile of v2, /device:TPU:8, one launch (start us, length us, event | category | flops | bytes accessed | tf_op | source)
XLA Modules:
  0.0 250.5 jit_solution(10639384531450750894)
XLA Ops:
  1.2 4.0 %pack.3 = (bf16[4,512,384]{2,1,0:T(8,128)(2,1)}, bf16[4,512,384]{2,1,0:T(8,128)(2,1)}) custom-call(s32[8]{0:T(128)} %compare_select_fusion.3.sc, s32[4]{0:T(128)} %off.27, bf16[512,1536]{1,0:T(8,128)(2,1)} %refs_1_.3, bf16[512,1536]{1,0:T(8,128)(2,1)} %refs_1_.3, bf16[512,1536]{1,0:T(8,128)(2,1)} %refs_3_.3, bf16[512,1536]{1,0:T(8,128)(2,1)} %refs_3_.3, ...), custom_call_target="tpu_custom_call" | custom-call | bytes 6291456 | tf_op jit(solution)/shard_map/pack/pallas_call | solution.py:102
  5.2 4.0 %pack.2 = (bf16[4,512,384]{2,1,0:T(8,128)(2,1)}, bf16[4,512,384]{2,1,0:T(8,128)(2,1)}) custom-call(s32[8]{0:T(128)} %compare_select_fusion.3.sc, s32[4]{0:T(128)} %off.27, bf16[512,1536]{1,0:T(8,128)(2,1)} %refs_1_.3, bf16[512,1536]{1,0:T(8,128)(2,1)} %refs_1_.3, bf16[512,1536]{1,0:T(8,128)(2,1)} %refs_3_.3, bf16[512,1536]{1,0:T(8,128)(2,1)} %refs_3_.3, ...), custom_call_target="tpu_custom_call" | custom-call | bytes 6291456 | tf_op jit(solution)/shard_map/pack/pallas_call | solution.py:102
  10.9 5.1 %halo.3 = (bf16[2,896,384]{2,1,0:T(8,128)(2,1)}, bf16[2,896,384]{2,1,0:T(8,128)(2,1)}) custom-call(s32[8]{0:T(128)} %compare_select_fusion.3.sc, s32[4]{0:T(128)} %off.27, bf16[4,512,384]{2,1,0:T(8,128)(2,1)} %get-tuple-element.51.own, bf16[4,512,384]{2,1,0:T(8,128)(2,1)} %copy-done.1), custom_call_target="tpu_custom_call" | custom-call | bytes 12582912 | tf_op jit(solution)/shard_map/halo/pallas_call | solution.py:138
  32.2 22.7 %collective-permute-done.4 = bf16[2,32,768]{2,1,0:T(8,128)(2,1)S(1)} collective-permute-done((bf16[2,32,768]{2,1,0:T(8,128)(2,1)}, bf16[2,32,768]{2,1,0:T(8,128)(2,1)S(1)}, u32[]{:S(2)}, u32[]{:S(2)}) %collective-permute-start.4) | collective-permute-done | bytes 98336 | tf_op jit(solution)/shard_map/ppermute | solution.py:531
  74.8 5.2 %halo.2 = (bf16[2,896,384]{2,1,0:T(8,128)(2,1)}, bf16[2,896,384]{2,1,0:T(8,128)(2,1)}) custom-call(s32[8]{0:T(128)} %compare_select_fusion.3.sc, s32[4]{0:T(128)} %off.27, bf16[4,512,384]{2,1,0:T(8,128)(2,1)} %get-tuple-element.33.own, bf16[4,512,384]{2,1,0:T(8,128)(2,1)} %copy-done), custom_call_target="tpu_custom_call" | custom-call | bytes 12582912 | tf_op jit(solution)/shard_map/halo/pallas_call | solution.py:138
  85.6 18.8 %attn.3 = (bf16[1024,384]{1,0:T(8,128)(2,1)}, f32[2,1024,384]{2,1,0:T(8,128)}, f32[3,8,1024]{2,1,0:T(8,128)}, bf16[2,512,384]{2,1,0:T(8,128)(2,1)}) custom-call(s32[8]{0:T(128)} %compare_select_fusion.3.sc, s32[4]{0:T(128)} %off.27, bf16[4,512,384]{2,1,0:T(8,128)(2,1)} %get-tuple-element.51.own, bf16[4,512,384]{2,1,0:T(8,128)(2,1)} %copy-done.1, ...), custom_call_target="tpu_custom_call" | custom-call | flops 12079595520 | bytes 12000000 | tf_op jit(solution)/shard_map/attn/pallas_call | solution.py:413
  105.7 4.2 %collective-permute-start.12 = (bf16[2,896,384]{2,1,0:T(8,128)(2,1)}, bf16[2,896,384]{2,1,0:T(8,128)(2,1)S(1)}, u32[]{:S(2)}, u32[]{:S(2)}) collective-permute-start(bf16[2,896,384]{2,1,0:T(8,128)(2,1)} %get-tuple-element.43), channel_id=1, source_target_pairs={{0,120},{4,124},{8,0},{12,4},{16,8},{20,12},{24,16},{28,20},{32,24... | collective-permute-start | bytes 4128776 | tf_op jit(solution)/shard_map/ppermute | solution.py:531
  109.8 4.2 %collective-permute-start.31 = (bf16[2,128,384]{2,1,0:T(8,128)(2,1)S(1)}, bf16[2,128,384]{2,1,0:T(8,128)(2,1)S(1)}, u32[]{:S(2)}, u32[]{:S(2)}) collective-permute-start(bf16[2,128,384]{2,1,0:T(8,128)(2,1)S(1)} %get-tuple-element.63), channel_id=1, source_target_pairs={{0,96},{4,100},{8,104},{12,108},{16,112},{20,116},{24,120},{28,124... | collective-permute-start | bytes 589832 | tf_op jit(solution)/shard_map/ppermute | solution.py:531
  114.0 10.6 %collective-permute-done.1.halo = bf16[2,896,384]{2,1,0:T(8,128)(2,1)S(1)} collective-permute-done((bf16[2,896,384]{2,1,0:T(8,128)(2,1)}, bf16[2,896,384]{2,1,0:T(8,128)(2,1)S(1)}, u32[]{:S(2)}, u32[]{:S(2)}) %collective-permute-start.1) | collective-permute-done | bytes 1376288 | tf_op jit(solution)/shard_map/ppermute | solution.py:531
  125.8 18.8 %attn.2 = (bf16[1024,384]{1,0:T(8,128)(2,1)}, f32[2,1024,384]{2,1,0:T(8,128)}, f32[3,8,1024]{2,1,0:T(8,128)}, bf16[2,512,384]{2,1,0:T(8,128)(2,1)}) custom-call(s32[8]{0:T(128)} %compare_select_fusion.3.sc, s32[4]{0:T(128)} %off.27, bf16[4,512,384]{2,1,0:T(8,128)(2,1)} %get-tuple-element.33.own, bf16[4,512,384]{2,1,0:T(8,128)(2,1)} %copy-done, ...), custom_call_target="tpu_custom_call" | custom-call | flops 12079595520 | bytes 12000000 | tf_op jit(solution)/shard_map/attn/pallas_call | solution.py:413
  144.7 8.0 %collective-permute-done.31 = bf16[2,128,384]{2,1,0:T(8,128)(2,1)S(1)} collective-permute-done((bf16[2,128,384]{2,1,0:T(8,128)(2,1)S(1)}, bf16[2,128,384]{2,1,0:T(8,128)(2,1)S(1)}, u32[]{:S(2)}, u32[]{:S(2)}) %collective-permute-start.31) | collective-permute-done | bytes 196640 | tf_op jit(solution)/shard_map/ppermute | solution.py:531
  152.7 4.2 %collective-permute-done.32 = bf16[2,128,384]{2,1,0:T(8,128)(2,1)S(1)} collective-permute-done((bf16[2,128,384]{2,1,0:T(8,128)(2,1)S(1)}, bf16[2,128,384]{2,1,0:T(8,128)(2,1)S(1)}, u32[]{:S(2)}, u32[]{:S(2)}) %collective-permute-start.32) | collective-permute-done | bytes 196640 | tf_op jit(solution)/shard_map/ppermute | solution.py:531
  160.5 5.0 %collective-permute-done.36.refs_3_ = bf16[2,128,384]{2,1,0:T(8,128)(2,1)S(1)} collective-permute-done((bf16[2,128,384]{2,1,0:T(8,128)(2,1)S(1)}, bf16[2,128,384]{2,1,0:T(8,128)(2,1)S(1)}, u32[]{:S(2)}, u32[]{:S(2)}) %collective-permute-start.36) | collective-permute-done | bytes 196640 | tf_op jit(solution)/shard_map/ppermute | solution.py:531
  165.5 3.6 %collective-permute-start.15 = (bf16[2,128,384]{2,1,0:T(8,128)(2,1)S(1)}, bf16[2,128,384]{2,1,0:T(8,128)(2,1)S(1)}, u32[]{:S(2)}, u32[]{:S(2)}) collective-permute-start(bf16[2,128,384]{2,1,0:T(8,128)(2,1)S(1)} %get-tuple-element.68), channel_id=1, source_target_pairs={{0,64},{4,68},{8,72},{12,76},{16,80},{20,84},{24,88},{28,92},{32,9... | collective-permute-start | bytes 589832 | tf_op jit(solution)/shard_map/ppermute | solution.py:531
  169.2 7.9 %later.3.dkv = f32[2,1024,384]{2,1,0:T(8,128)} custom-call(s32[8]{0:T(128)} %compare_select_fusion.3.sc, s32[4]{0:T(128)} %off.27, bf16[4,512,384]{2,1,0:T(8,128)(2,1)} %get-tuple-element.51.own, bf16[4,512,384]{2,1,0:T(8,128)(2,1)} %copy-done.1, bf16[2,896,384]{2,1,0:T(8,128)(2,1)} %copy-done.3, f32[3,8,1024]{2,1,0:T(8,128)} %copy-done.26, ...), custom_call_target="tpu_custom_call" | custom-call | flops 2818572288 | bytes 12000000 | tf_op jit(solution)/shard_map/later/pallas_call | solution.py:382
  177.7 5.2 %finish.3 = (bf16[2,3,128,384]{3,2,1,0:T(8,128)(2,1)}, bf16[2,3,128,384]{3,2,1,0:T(8,128)(2,1)}, bf16[2,3,128,384]{3,2,1,0:T(8,128)(2,1)}, bf16[2,3,128,384]{3,2,1,0:T(8,128)(2,1)}) custom-call(s32[8]{0:T(128)} %compare_select_fusion.3.sc, s32[4]{0:T(128)} %off.27, bf16[1024,384]{1,0:T(8,128)(2,1)} %get-tuple-element.54.dq, f32[2,1024,384]{2,1,0:T(8,128)} %later.3.dkv, ...), custom_call_target="tpu_custom_call" | custom-call | bytes 7864320 | tf_op jit(solution)/shard_map/finish/pallas_call | solution.py:470
  184.6 3.3 %collective-permute-start.19 = (bf16[2,128,384]{2,1,0:T(8,128)(2,1)S(1)}, bf16[2,128,384]{2,1,0:T(8,128)(2,1)S(1)}, u32[]{:S(2)}, u32[]{:S(2)}) collective-permute-start(bf16[2,128,384]{2,1,0:T(8,128)(2,1)S(1)} %add_convert_fusion.1.refs_0_), channel_id=1, source_target_pairs={{0,24},{4,28},{8,0},{12,4},{16,8},{20,12},{24,16},{28,20},{32,56},... | collective-permute-start | bytes 589832 | tf_op jit(solution)/shard_map/ppermute | solution.py:531
  196.7 7.8 %later.2.dkv = f32[2,1024,384]{2,1,0:T(8,128)} custom-call(s32[8]{0:T(128)} %compare_select_fusion.3.sc, s32[4]{0:T(128)} %off.27, bf16[4,512,384]{2,1,0:T(8,128)(2,1)} %get-tuple-element.33.own, bf16[4,512,384]{2,1,0:T(8,128)(2,1)} %copy-done, bf16[2,896,384]{2,1,0:T(8,128)(2,1)} %copy-done.2, f32[3,8,1024]{2,1,0:T(8,128)} %copy-done.27, ...), custom_call_target="tpu_custom_call" | custom-call | flops 2818572288 | bytes 12000000 | tf_op jit(solution)/shard_map/later/pallas_call | solution.py:382
  205.2 5.1 %finish.2 = (bf16[2,3,128,384]{3,2,1,0:T(8,128)(2,1)}, bf16[2,3,128,384]{3,2,1,0:T(8,128)(2,1)}, bf16[2,3,128,384]{3,2,1,0:T(8,128)(2,1)}, bf16[2,3,128,384]{3,2,1,0:T(8,128)(2,1)}) custom-call(s32[8]{0:T(128)} %compare_select_fusion.3.sc, s32[4]{0:T(128)} %off.27, bf16[1024,384]{1,0:T(8,128)(2,1)} %get-tuple-element.42.dq, f32[2,1024,384]{2,1,0:T(8,128)} %later.2.dkv, ...), custom_call_target="tpu_custom_call" | custom-call | bytes 7864320 | tf_op jit(solution)/shard_map/finish/pallas_call | solution.py:470
  215.3 8.0 %collective-permute-done.39.refs_8_ = bf16[2,3,128,384]{3,2,1,0:T(8,128)(2,1)S(1)} collective-permute-done((bf16[2,3,128,384]{3,2,1,0:T(8,128)(2,1)}, bf16[2,3,128,384]{3,2,1,0:T(8,128)(2,1)S(1)}, u32[]{:S(2)}, u32[]{:S(2)}) %collective-permute-start.39) | collective-permute-done | bytes 589856 | tf_op jit(solution)/shard_map/ppermute | solution.py:531
  224.2 10.6 %collective-permute-done.20.refs_1_ = bf16[2,3,128,384]{3,2,1,0:T(8,128)(2,1)S(1)} collective-permute-done((bf16[2,3,128,384]{3,2,1,0:T(8,128)(2,1)}, bf16[2,3,128,384]{3,2,1,0:T(8,128)(2,1)S(1)}, u32[]{:S(2)}, u32[]{:S(2)}) %collective-permute-start.20) | collective-permute-done | bytes 589856 | tf_op jit(solution)/shard_map/ppermute | solution.py:531
  234.8 5.3 %collective-permute-done.22.refs_3_ = bf16[2,3,128,384]{3,2,1,0:T(8,128)(2,1)S(1)} collective-permute-done((bf16[2,3,128,384]{3,2,1,0:T(8,128)(2,1)}, bf16[2,3,128,384]{3,2,1,0:T(8,128)(2,1)S(1)}, u32[]{:S(2)}, u32[]{:S(2)}) %collective-permute-start.22) | collective-permute-done | bytes 589856 | tf_op jit(solution)/shard_map/ppermute | solution.py:531
  241.0 2.8 %collective-permute-done.23.refs_4_ = bf16[4,3,128,384]{3,2,1,0:T(8,128)(2,1)S(1)} collective-permute-done((bf16[4,3,128,384]{3,2,1,0:T(8,128)(2,1)S(1)}, bf16[4,3,128,384]{3,2,1,0:T(8,128)(2,1)S(1)}, u32[]{:S(2)}, u32[]{:S(2)}) %collective-permute-start.23) | collective-permute-done | bytes 1179680 | tf_op jit(solution)/shard_map/ppermute | solution.py:531
  244.8 5.7 %place.1 = (bf16[128,6144]{1,0:T(8,128)(2,1)}, bf16[128,6144]{1,0:T(8,128)(2,1)}, bf16[128,6144]{1,0:T(8,128)(2,1)}) custom-call(s32[8]{0:T(128)} %compare_select_fusion.3.sc, s32[4]{0:T(128)} %off.27, bf16[2,3,128,384]{3,2,1,0:T(8,128)(2,1)} %get-tuple-element.47.refs_0_, bf16[2,3,128,384]{3,2,1,0:T(8,128)(2,1)} %copy-done.8, ...), custom_call_target="tpu_custom_call" | custom-call | bytes 9437184 | tf_op jit(solution)/shard_map/place/pallas_call | solution.py:515
  (174 shorter events, 68.5 us)
Async XLA Ops:
  9.3 64.4 %collective-permute-start = (bf16[4,512,384]{2,1,0:T(8,128)(2,1)}, bf16[4,512,384]{2,1,0:T(8,128)(2,1)S(1)}, u32[]{:S(2)}, u32[]{:S(2)}) collective-permute-start(bf16[4,512,384]{2,1,0:T(8,128)(2,1)} %get-tuple-element.34), channel_id=1, source_target_pairs={{0,4},{4,0},{8,12},{12,8},{16,20},{20,16},{24,28},{28,24},{32,36},... | collective-permute-start | bytes 4718600 | tf_op jit(solution)/shard_map/ppermute | solution.py:531
  16.0 69.6 %collective-permute-start.25 = (bf16[2,896,384]{2,1,0:T(8,128)(2,1)}, bf16[2,896,384]{2,1,0:T(8,128)(2,1)}, u32[]{:S(2)}, u32[]{:S(2)}) collective-permute-start(bf16[2,896,384]{2,1,0:T(8,128)(2,1)} %get-tuple-element.53), channel_id=1, source_target_pairs={{0,8},{4,12},{8,16},{12,20},{16,24},{20,28},{24,32},{28,36},{32,40... | collective-permute-start | bytes 4128776 | tf_op jit(solution)/shard_map/ppermute | solution.py:531
  28.2 26.6 %collective-permute-start.4 = (bf16[2,32,768]{2,1,0:T(8,128)(2,1)}, bf16[2,32,768]{2,1,0:T(8,128)(2,1)S(1)}, u32[]{:S(2)}, u32[]{:S(2)}) collective-permute-start(bf16[2,32,768]{2,1,0:T(8,128)(2,1)} %get-tuple-element.39), channel_id=1, source_target_pairs={{0,16},{4,20},{8,24},{12,28},{16,0},{20,4},{24,8},{28,12},{32,48},... | collective-permute-start | bytes 294920 | tf_op jit(solution)/shard_map/ppermute | solution.py:531
  29.9 25.0 %collective-permute-start.5 = (bf16[2,32,768]{2,1,0:T(8,128)(2,1)}, bf16[2,32,768]{2,1,0:T(8,128)(2,1)S(1)}, u32[]{:S(2)}, u32[]{:S(2)}) collective-permute-start(bf16[2,32,768]{2,1,0:T(8,128)(2,1)} %get-tuple-element.40), channel_id=1, source_target_pairs={{0,8},{4,12},{8,16},{12,20},{16,24},{20,28},{24,0},{28,4},{32,40},... | collective-permute-start | bytes 294920 | tf_op jit(solution)/shard_map/ppermute | solution.py:531
  73.7 32.0 %collective-permute-start.11 = (bf16[2,128,384]{2,1,0:T(8,128)(2,1)S(1)}, bf16[2,128,384]{2,1,0:T(8,128)(2,1)S(1)}, u32[]{:S(2)}, u32[]{:S(2)}) collective-permute-start(bf16[2,128,384]{2,1,0:T(8,128)(2,1)S(1)} %get-tuple-element.70.s0), channel_id=1, source_target_pairs={{0,96},{4,100},{8,104},{12,108},{16,112},{20,116},{24,120},{28,124... | collective-permute-start | bytes 589832 | tf_op jit(solution)/shard_map/ppermute | solution.py:531
  80.1 29.8 %collective-permute-start.10 = (bf16[2,128,384]{2,1,0:T(8,128)(2,1)S(1)}, bf16[2,128,384]{2,1,0:T(8,128)(2,1)S(1)}, u32[]{:S(2)}, u32[]{:S(2)}) collective-permute-start(bf16[2,128,384]{2,1,0:T(8,128)(2,1)S(1)} %get-tuple-element.70.s0), channel_id=1, source_target_pairs={{0,64},{4,68},{8,72},{12,76},{16,80},{20,84},{24,88},{28,92},{32,9... | collective-permute-start | bytes 589832 | tf_op jit(solution)/shard_map/ppermute | solution.py:531
  82.3 31.7 %collective-permute-start.9 = (bf16[2,128,384]{2,1,0:T(8,128)(2,1)S(1)}, bf16[2,128,384]{2,1,0:T(8,128)(2,1)S(1)}, u32[]{:S(2)}, u32[]{:S(2)}) collective-permute-start(bf16[2,128,384]{2,1,0:T(8,128)(2,1)S(1)} %get-tuple-element.70.s0), channel_id=1, source_target_pairs={{0,32},{4,36},{8,40},{12,44},{16,48},{20,52},{24,56},{28,60},{32,6... | collective-permute-start | bytes 589832 | tf_op jit(solution)/shard_map/ppermute | solution.py:531
  83.1 75.1 %collective-permute-start.29 = (bf16[2,896,384]{2,1,0:T(8,128)(2,1)S(1)}, bf16[2,896,384]{2,1,0:T(8,128)(2,1)S(1)}, u32[]{:S(2)}, u32[]{:S(2)}) collective-permute-start(bf16[2,896,384]{2,1,0:T(8,128)(2,1)S(1)} %copy-done.32), channel_id=1, source_target_pairs={{0,120},{4,124},{8,0},{12,4},{16,8},{20,12},{24,16},{28,20},{32,24... | collective-permute-start | bytes 4128776 | tf_op jit(solution)/shard_map/ppermute | solution.py:531
  85.6 39.1 %collective-permute-start.1 = (bf16[2,896,384]{2,1,0:T(8,128)(2,1)}, bf16[2,896,384]{2,1,0:T(8,128)(2,1)S(1)}, u32[]{:S(2)}, u32[]{:S(2)}) collective-permute-start(bf16[2,896,384]{2,1,0:T(8,128)(2,1)} %get-tuple-element.35), channel_id=1, source_target_pairs={{0,8},{4,12},{8,16},{12,20},{16,24},{20,28},{24,32},{28,36},{32,40... | collective-permute-start | bytes 4128776 | tf_op jit(solution)/shard_map/ppermute | solution.py:531
  105.7 83.1 %collective-permute-start.12 = (bf16[2,896,384]{2,1,0:T(8,128)(2,1)}, bf16[2,896,384]{2,1,0:T(8,128)(2,1)S(1)}, u32[]{:S(2)}, u32[]{:S(2)}) collective-permute-start(bf16[2,896,384]{2,1,0:T(8,128)(2,1)} %get-tuple-element.43), channel_id=1, source_target_pairs={{0,120},{4,124},{8,0},{12,4},{16,8},{20,12},{24,16},{28,20},{32,24... | collective-permute-start | bytes 4128776 | tf_op jit(solution)/shard_map/ppermute | solution.py:531
  109.8 42.8 %collective-permute-start.31 = (bf16[2,128,384]{2,1,0:T(8,128)(2,1)S(1)}, bf16[2,128,384]{2,1,0:T(8,128)(2,1)S(1)}, u32[]{:S(2)}, u32[]{:S(2)}) collective-permute-start(bf16[2,128,384]{2,1,0:T(8,128)(2,1)S(1)} %get-tuple-element.63), channel_id=1, source_target_pairs={{0,96},{4,100},{8,104},{12,108},{16,112},{20,116},{24,120},{28,124... | collective-permute-start | bytes 589832 | tf_op jit(solution)/shard_map/ppermute | solution.py:531
  114.0 38.7 %collective-permute-start.33 = (bf16[2,128,384]{2,1,0:T(8,128)(2,1)S(1)}, bf16[2,128,384]{2,1,0:T(8,128)(2,1)S(1)}, u32[]{:S(2)}, u32[]{:S(2)}) collective-permute-start(bf16[2,128,384]{2,1,0:T(8,128)(2,1)S(1)} %get-tuple-element.64), channel_id=1, source_target_pairs={{0,32},{4,36},{8,40},{12,44},{16,48},{20,52},{24,56},{28,60},{32,6... | collective-permute-start | bytes 589832 | tf_op jit(solution)/shard_map/ppermute | solution.py:531
  124.7 32.3 %collective-permute-start.32 = (bf16[2,128,384]{2,1,0:T(8,128)(2,1)S(1)}, bf16[2,128,384]{2,1,0:T(8,128)(2,1)S(1)}, u32[]{:S(2)}, u32[]{:S(2)}) collective-permute-start(bf16[2,128,384]{2,1,0:T(8,128)(2,1)S(1)} %get-tuple-element.65), channel_id=1, source_target_pairs={{0,64},{4,68},{8,72},{12,76},{16,80},{20,84},{24,88},{28,92},{32,9... | collective-permute-start | bytes 589832 | tf_op jit(solution)/shard_map/ppermute | solution.py:531
  158.2 26.2 %collective-permute-start.14 = (bf16[2,128,384]{2,1,0:T(8,128)(2,1)S(1)}, bf16[2,128,384]{2,1,0:T(8,128)(2,1)S(1)}, u32[]{:S(2)}, u32[]{:S(2)}) collective-permute-start(bf16[2,128,384]{2,1,0:T(8,128)(2,1)S(1)} %get-tuple-element.66), channel_id=1, source_target_pairs={{0,96},{4,100},{8,104},{12,108},{16,112},{20,116},{24,120},{28,124... | collective-permute-start | bytes 589832 | tf_op jit(solution)/shard_map/ppermute | solution.py:531
  160.5 23.9 %collective-permute-start.16 = (bf16[2,128,384]{2,1,0:T(8,128)(2,1)S(1)}, bf16[2,128,384]{2,1,0:T(8,128)(2,1)S(1)}, u32[]{:S(2)}, u32[]{:S(2)}) collective-permute-start(bf16[2,128,384]{2,1,0:T(8,128)(2,1)S(1)} %get-tuple-element.67), channel_id=1, source_target_pairs={{0,32},{4,36},{8,40},{12,44},{16,48},{20,52},{24,56},{28,60},{32,6... | collective-permute-start | bytes 589832 | tf_op jit(solution)/shard_map/ppermute | solution.py:531
  165.5 18.9 %collective-permute-start.15 = (bf16[2,128,384]{2,1,0:T(8,128)(2,1)S(1)}, bf16[2,128,384]{2,1,0:T(8,128)(2,1)S(1)}, u32[]{:S(2)}, u32[]{:S(2)}) collective-permute-start(bf16[2,128,384]{2,1,0:T(8,128)(2,1)S(1)} %get-tuple-element.68), channel_id=1, source_target_pairs={{0,64},{4,68},{8,72},{12,76},{16,80},{20,84},{24,88},{28,92},{32,9... | collective-permute-start | bytes 589832 | tf_op jit(solution)/shard_map/ppermute | solution.py:531
  182.9 29.8 %collective-permute-start.37 = (bf16[2,3,128,384]{3,2,1,0:T(8,128)(2,1)}, bf16[2,3,128,384]{3,2,1,0:T(8,128)(2,1)S(1)}, u32[]{:S(2)}, u32[]{:S(2)}) collective-permute-start(bf16[2,3,128,384]{3,2,1,0:T(8,128)(2,1)} %get-tuple-element.60), channel_id=1, source_target_pairs={{0,1},{1,2},{2,3},{3,0},{4,5},{5,6},{6,7},{7,4},{8,9},{9,10},{10,1... | collective-permute-start | bytes 1769480 | tf_op jit(solution)/shard_map/ppermute | solution.py:531
  187.9 16.6 %collective-permute-start.18 = (bf16[2,128,384]{2,1,0:T(8,128)(2,1)S(1)}, bf16[2,128,384]{2,1,0:T(8,128)(2,1)S(1)}, u32[]{:S(2)}, u32[]{:S(2)}) collective-permute-start(bf16[2,128,384]{2,1,0:T(8,128)(2,1)S(1)} %add_convert_fusion.1.refs_0_), channel_id=1, source_target_pairs={{0,16},{4,20},{8,24},{12,28},{16,0},{20,4},{24,8},{28,12},{32,48},... | collective-permute-start | bytes 589832 | tf_op jit(solution)/shard_map/ppermute | solution.py:531
  192.5 22.8 %collective-permute-start.38 = (bf16[2,3,128,384]{3,2,1,0:T(8,128)(2,1)}, bf16[2,3,128,384]{3,2,1,0:T(8,128)(2,1)S(1)}, u32[]{:S(2)}, u32[]{:S(2)}) collective-permute-start(bf16[2,3,128,384]{3,2,1,0:T(8,128)(2,1)} %get-tuple-element.61), channel_id=1, source_target_pairs={{0,2},{1,3},{2,0},{3,1},{4,6},{5,7},{6,4},{7,5},{8,10},{9,11},{10,... | collective-permute-start | bytes 1769480 | tf_op jit(solution)/shard_map/ppermute | solution.py:531
  195.2 28.1 %collective-permute-start.39 = (bf16[2,3,128,384]{3,2,1,0:T(8,128)(2,1)}, bf16[2,3,128,384]{3,2,1,0:T(8,128)(2,1)S(1)}, u32[]{:S(2)}, u32[]{:S(2)}) collective-permute-start(bf16[2,3,128,384]{3,2,1,0:T(8,128)(2,1)} %get-tuple-element.62), channel_id=1, source_target_pairs={{0,3},{1,0},{2,1},{3,2},{4,7},{5,4},{6,5},{7,6},{8,11},{9,8},{10,9... | collective-permute-start | bytes 1769480 | tf_op jit(solution)/shard_map/ppermute | solution.py:531
  210.4 24.3 %collective-permute-start.20 = (bf16[2,3,128,384]{3,2,1,0:T(8,128)(2,1)}, bf16[2,3,128,384]{3,2,1,0:T(8,128)(2,1)S(1)}, u32[]{:S(2)}, u32[]{:S(2)}) collective-permute-start(bf16[2,3,128,384]{3,2,1,0:T(8,128)(2,1)} %get-tuple-element.48), channel_id=1, source_target_pairs={{0,1},{1,2},{2,3},{3,0},{4,5},{5,6},{6,7},{7,4},{8,9},{9,10},{10,1... | collective-permute-start | bytes 1769480 | tf_op jit(solution)/shard_map/ppermute | solution.py:531
  211.0 23.8 %collective-permute-start.21 = (bf16[2,3,128,384]{3,2,1,0:T(8,128)(2,1)}, bf16[2,3,128,384]{3,2,1,0:T(8,128)(2,1)S(1)}, u32[]{:S(2)}, u32[]{:S(2)}) collective-permute-start(bf16[2,3,128,384]{3,2,1,0:T(8,128)(2,1)} %get-tuple-element.49), channel_id=1, source_target_pairs={{0,2},{1,3},{2,0},{3,1},{4,6},{5,7},{6,4},{7,5},{8,10},{9,11},{10,... | collective-permute-start | bytes 1769480 | tf_op jit(solution)/shard_map/ppermute | solution.py:531
  212.8 27.4 %collective-permute-start.22 = (bf16[2,3,128,384]{3,2,1,0:T(8,128)(2,1)}, bf16[2,3,128,384]{3,2,1,0:T(8,128)(2,1)S(1)}, u32[]{:S(2)}, u32[]{:S(2)}) collective-permute-start(bf16[2,3,128,384]{3,2,1,0:T(8,128)(2,1)} %get-tuple-element.50), channel_id=1, source_target_pairs={{0,3},{1,0},{2,1},{3,2},{4,7},{5,4},{6,5},{7,6},{8,11},{9,8},{10,9... | collective-permute-start | bytes 1769480 | tf_op jit(solution)/shard_map/ppermute | solution.py:531
  224.2 16.8 %collective-permute-start.40 = (bf16[4,3,128,384]{3,2,1,0:T(8,128)(2,1)S(1)}, bf16[4,3,128,384]{3,2,1,0:T(8,128)(2,1)S(1)}, u32[]{:S(2)}, u32[]{:S(2)}) collective-permute-start(bf16[4,3,128,384]{3,2,1,0:T(8,128)(2,1)S(1)} %pad_maximum_fusion.1), channel_id=1, source_target_pairs={{0,4},{4,0},{8,12},{12,8},{16,20},{20,16},{24,28},{28,24},{32,36},... | collective-permute-start | bytes 3538952 | tf_op jit(solution)/shard_map/ppermute | solution.py:531
  (59 other events, 481.1 us)

commit v3 on v2

--- a/solution.py
+++ b/solution.py
@@ -447,8 +447,10 @@
     )(sc, off, own, recv, halo, *sums)
 
 
-def finish_kernel(sc, off, dq, dkv, *refs):
-    tots, outs = refs[:SIDE], refs[SIDE:]
+def finish_kernel(sc, off, dkv, *refs):
+    tots, rest = refs[:SIDE], refs[SIDE:]
+    dqs, outs = rest[:-SIDE], rest[-SIDE:]
+    lead = len(dqs)
     core, y, z, x = sc[1], sc[2], sc[3], sc[4]
     local = off[y] & 7
     here = (off[y] >> 3) == z
@@ -460,33 +462,60 @@
             block = ((core + side) & 1) * SIDE + ((x + step) & 3)
             rows = pl.ds(pl.multiple_of(block * BLOCK, BLOCK), BLOCK)
             value = dkv[:, rows, :] + jnp.where(here & (local == block), total, 0.0)
-            outs[step][side, 0] = dq[rows, :]
-            outs[step][side, 1:3] = value.astype(BF16)
-
-
-def finish(sc, off, dq, dkv, tots):
-    width = dq.shape[1]
-    shape = (2, 3, BLOCK, width)
+            for dq in dqs:
+                outs[step][side, 0] = dq[rows, :]
+            outs[step][side, lead : lead + 2] = value.astype(BF16)
+
+
+def finish(sc, off, dkv, tots, dqs=()):
+    width = dkv.shape[2]
+    shape = (2, 2 + len(dqs), BLOCK, width)
     return pl.pallas_call(
         finish_kernel,
         grid_spec=pltpu.PrefetchScalarGridSpec(
             num_scalar_prefetch=2,
             grid=(width // HDIM,),
             in_specs=[
-                pl.BlockSpec((OWN, HDIM), lambda h, sc, off: (0, h)),
                 pl.BlockSpec((2, OWN, HDIM), lambda h, sc, off: (0, 0, h)),
             ]
-            + [pl.BlockSpec((2, BLOCK, HDIM), lambda h, sc, off: (0, 0, h))] * SIDE,
-            out_specs=[pl.BlockSpec((2, 3, BLOCK, HDIM), lambda h, sc, off: (0, 0, 0, h))] * SIDE,
+            + [pl.BlockSpec((2, BLOCK, HDIM), lambda h, sc, off: (0, 0, h))] * SIDE
+            + [pl.BlockSpec((OWN, HDIM), lambda h, sc, off: (0, h))] * len(dqs),
+            out_specs=[pl.BlockSpec((*shape[:3], HDIM), lambda h, sc, off: (0, 0, 0, h))] * SIDE,
         ),
         out_shape=[jax.ShapeDtypeStruct(shape, BF16)] * SIDE,
         compiler_params=params(),
         cost_estimate=cost(0, 20 * OWN * width),
         name="finish",
-    )(sc, off, dq, dkv, *tots)
-
-
-def place_kernel(sc, off, *refs):
+    )(sc, off, dkv, *tots, *dqs)
+
+
+def cut_kernel(sc, off, dq, *outs):
+    core, x = sc[1], sc[4]
+    for step in range(SIDE):
+        for side in range(2):
+            block = ((core + side) & 1) * SIDE + ((x + step) & 3)
+            rows = pl.ds(pl.multiple_of(block * BLOCK, BLOCK), BLOCK)
+            outs[step][side, 0] = dq[rows, :]
+
+
+def cut(sc, off, dq):
+    shape = (2, 1, BLOCK, dq.shape[1])
+    return pl.pallas_call(
+        cut_kernel,
+        grid_spec=pltpu.PrefetchScalarGridSpec(
+            num_scalar_prefetch=2,
+            grid=(1,),
+            in_specs=[whole(dq.shape)],
+            out_specs=[whole(shape)] * SIDE,
+        ),
+        out_shape=[jax.ShapeDtypeStruct(shape, BF16)] * SIDE,
+        compiler_params=params(),
+        cost_estimate=cost(0, 4 * OWN * shape[3]),
+        name="cut",
+    )(sc, off, dq)
+
+
+def place_kernel(slots, sc, off, *refs):
     groups = len(SIZES)
     outs = refs[(SIDE + 1) * groups :]
     x, core = sc[4], sc[1]
@@ -500,31 +529,38 @@
                 side = core if part == 0 else 1 - core
                 first = pl.multiple_of(((source * 2 + side) * heads + at) * HDIM, HDIM)
                 ref = refs[g * (SIDE + 1) + (step if part == 0 else SIDE)]
-                for n in range(3):
-                    outs[n][:, pl.ds(first, width)] = ref[0 if part == 0 else step, n]
+                for n, out in enumerate(outs):
+                    out[:, pl.ds(first, width)] = ref[0 if part == 0 else step, slots[g] + n]
         at += SIZES[g]
 
 
-def place(sc, off, parts):
+def place(sc, off, parts, count, slots):
     columns = sum(SIZES) * HDIM * 2 * SIDE
     shape = (BLOCK, columns)
     specs = []
     for n, p in enumerate(parts):
         lead = SIDE if n % (SIDE + 1) == SIDE else 1
-        specs.append(pl.BlockSpec((lead, *p.shape[1:]), lambda i, sc, off: (0, 0, 0, 0)))
-    return pl.pallas_call(
-        place_kernel,
+        used = min(p.shape[1], slots[n // (SIDE + 1)] + count)
+        specs.append(pl.BlockSpec((lead, used, *p.shape[2:]), lambda i, sc, off: (0, 0, 0, 0)))
+    return pl.pallas_call(
+        functools.partial(place_kernel, slots),
         grid_spec=pltpu.PrefetchScalarGridSpec(
             num_scalar_prefetch=2,
             grid=(1,),
             in_specs=specs,
-            out_specs=[whole(shape)] * 3,
-        ),
-        out_shape=[jax.ShapeDtypeStruct(shape, BF16)] * 3,
-        compiler_params=params(),
-        cost_estimate=cost(0, 12 * BLOCK * columns),
+            out_specs=[whole(shape)] * count,
+        ),
+        out_shape=[jax.ShapeDtypeStruct(shape, BF16)] * count,
+        compiler_params=params(),
+        cost_estimate=cost(0, 4 * count * BLOCK * columns),
         name="place",
     )(sc, off, *parts)
+
+
+def spread_out(cuts):
+    there = [cuts[0]]
+    there += [named(cuts[n], along_x(n), "tp") for n in range(1, SIDE)]
+    return there + [named(jnp.concatenate([t[1:] for t in there], axis=0), SWAP)]
 
 
 def named(value, pairs, axis="ctx"):
@@ -561,7 +597,7 @@
         qd, kv = halo_of(sc, off, own, recv)
         work.append((own, recv, named(kv, ring(1)), named(qd, ring(-1))))
 
-    parts = []
+    dqs, dkvs, totals = [], [], []
     for g, heads in enumerate(SIZES):
         own, recv, kv, qd = work[g]
         mine = summary[:, :, bases[g] * HDIM : (bases[g] + heads) * HDIM]
@@ -574,13 +610,18 @@
             moved = named(sent[:, n * BLOCK : (n + 1) * BLOCK], along_y(-n))
             part = part + moved.astype(F32)
         part = part.astype(BF16)
-        tots = [part] + [named(part, along_z(n)) for n in range(1, SIDE)]
-        cuts = finish(sc, off, dq, dkv, tots)
-        there = [cuts[0]]
-        there += [named(cuts[n], along_x(n), "tp") for n in range(1, SIDE)]
-        parts += there
-        parts.append(named(jnp.concatenate([t[1:] for t in there], axis=0), SWAP))
-    return tuple(place(sc, off, parts))
+        totals.append([part] + [named(part, along_z(n)) for n in range(1, SIDE)])
+        dqs.append(dq)
+        dkvs.append(dkv)
+    cuts = cut(sc, off, dqs[0])
+    first_q = spread_out(cuts)
+    cuts = finish(sc, off, dkvs[0], totals[0], (dqs[1],))
+    mixed = spread_out(cuts)
+    cuts = finish(sc, off, dkvs[1], totals[1])
+    last = spread_out(cuts)
+    grad_q = place(sc, off, first_q + mixed, 1, (0, 0))
+    grads = place(sc, off, mixed + last, 2, (1, 0))
+    return (*grad_q, *grads)
 
 
 def solution(mesh):

time: 256 us -> 262 us (1.023); the launches traced: 250 us -> 260 us
  starting transfers between devices: 50.4 us -> 57 us
  waiting for transfers between devices: 88 us -> 83 us
  Pallas kernels: 95.5 us -> 100 us
    ppermute x41 -> x45, starting transfers between devices: 50.4 us -> 57 us  [named(): return lax.ppermute(value, axis, pairs)]
    pallas_call x1 -> x3, Pallas kernels: 5.65 us -> 10.9 us  [the longest x2 8.15 us: place(): pl.pallas_call(functools.partial(place_kernel, slots), grid_spec=pltpu.Pr...]
    ppermute x41 -> x45, waiting for transfers between devices: 88 us -> 83 us  [named(): return lax.ppermute(value, axis, pairs)]
    unnamed x84 -> x92, local copies, waits for them, and re-layouts: 7.74 us -> 8.39 us
  transfers between devices with their start and end apart: 41 -> 45, of which waited for: 14 -> 13; matrix products, arithmetic and copies ran while one was open for 3% -> 3% of each run, Pallas kernels for 34% -> 36%
where the time goes in v3:
time: 262 us; the launch traced here: 260 us
  Pallas kernels  100 us (38%)
  waiting for transfers between devices  83 us (32%)
  starting transfers between devices  57 us (22%)
  local copies, waits for them, and re-layouts  13.5 us (5%)
  other arithmetic  3.89 us (1%)
    ppermute x45, waiting for transfers between devices, named(): return lax.ppermute(value, axis, pairs)  83 us
    ppermute x45, starting transfers between devices, named(): return lax.ppermute(value, axis, pairs)  57 us
    pallas_call x2, Pallas kernels, attn(): pl.pallas_call(attn_kernel, grid_spec=pltpu.PrefetchScalarGridSpec(num_sc...  37.7 us
    pallas_call x2, Pallas kernels, later(): pl.pallas_call(later_kernel, grid_spec=pltpu.PrefetchScalarGridSpec(num_s...  15.7 us
    pallas_call x2, Pallas kernels, halo_of(): pl.pallas_call(halo_kernel, grid_spec=pltpu.PrefetchScalarGridSpec(num_sc...  10.2 us
    pallas_call x2, Pallas kernels, finish(): pl.pallas_call(finish_kernel, grid_spec=pltpu.PrefetchScalarGridSpec(num_...  9.91 us
    unnamed x92, local copies, waits for them, and re-layouts  8.39 us
    pallas_call x2, Pallas kernels, place(): pl.pallas_call(functools.partial(place_kernel, slots), grid_spec=pltpu.Pr...  8.15 us
  transfers between devices with their start and end apart: 45, of which 13 were waited for; matrix products, arithmetic and copies ran while one was open for 3% of the time, Pallas kernels for 36%

profile of v3, /device:TPU:8, one launch (start us, length us, event | category | flops | bytes accessed | tf_op | source)
XLA Modules:
  0.0 259.6 jit_solution(16662555876854413737)
XLA Ops:
  1.2 4.0 %pack.2 = (bf16[4,512,384]{2,1,0:T(8,128)(2,1)}, bf16[4,512,384]{2,1,0:T(8,128)(2,1)}) custom-call(s32[8]{0:T(128)} %compare_select_fusion.3.sc, s32[4]{0:T(128)} %off.31, bf16[512,1536]{1,0:T(8,128)(2,1)} %refs_1_.3, bf16[512,1536]{1,0:T(8,128)(2,1)} %refs_1_.3, bf16[512,1536]{1,0:T(8,128)(2,1)} %refs_3_.3, bf16[512,1536]{1,0:T(8,128)(2,1)} %refs_3_.3, ...), custom_call_target="tpu_custom_call" | custom-call | bytes 6291456 | tf_op jit(solution)/shard_map/pack/pallas_call | solution.py:102
  5.2 4.0 %pack.3 = (bf16[4,512,384]{2,1,0:T(8,128)(2,1)}, bf16[4,512,384]{2,1,0:T(8,128)(2,1)}) custom-call(s32[8]{0:T(128)} %compare_select_fusion.3.sc, s32[4]{0:T(128)} %off.31, bf16[512,1536]{1,0:T(8,128)(2,1)} %refs_1_.3, bf16[512,1536]{1,0:T(8,128)(2,1)} %refs_1_.3, bf16[512,1536]{1,0:T(8,128)(2,1)} %refs_3_.3, bf16[512,1536]{1,0:T(8,128)(2,1)} %refs_3_.3, ...), custom_call_target="tpu_custom_call" | custom-call | bytes 6291456 | tf_op jit(solution)/shard_map/pack/pallas_call | solution.py:102
  10.8 5.1 %halo.2 = (bf16[2,896,384]{2,1,0:T(8,128)(2,1)}, bf16[2,896,384]{2,1,0:T(8,128)(2,1)}) custom-call(s32[8]{0:T(128)} %compare_select_fusion.3.sc, s32[4]{0:T(128)} %off.31, bf16[4,512,384]{2,1,0:T(8,128)(2,1)} %get-tuple-element.39.own, bf16[4,512,384]{2,1,0:T(8,128)(2,1)} %copy-done.1), custom_call_target="tpu_custom_call" | custom-call | bytes 12582912 | tf_op jit(solution)/shard_map/halo/pallas_call | solution.py:138
  32.0 22.7 %collective-permute-done.4 = bf16[2,32,768]{2,1,0:T(8,128)(2,1)S(1)} collective-permute-done((bf16[2,32,768]{2,1,0:T(8,128)(2,1)}, bf16[2,32,768]{2,1,0:T(8,128)(2,1)S(1)}, u32[]{:S(2)}, u32[]{:S(2)}) %collective-permute-start.4) | collective-permute-done | bytes 98336 | tf_op jit(solution)/shard_map/ppermute | solution.py:567
  59.0 4.3 %collective-permute-done.6.refs_1_ = bf16[2,32,768]{2,1,0:T(8,128)(2,1)S(1)} collective-permute-done((bf16[2,32,768]{2,1,0:T(8,128)(2,1)S(1)}, bf16[2,32,768]{2,1,0:T(8,128)(2,1)S(1)}, u32[]{:S(2)}, u32[]{:S(2)}) %collective-permute-start.6) | collective-permute-done | bytes 98336 | tf_op jit(solution)/shard_map/ppermute | solution.py:567
  75.1 5.2 %halo.3 = (bf16[2,896,384]{2,1,0:T(8,128)(2,1)}, bf16[2,896,384]{2,1,0:T(8,128)(2,1)}) custom-call(s32[8]{0:T(128)} %compare_select_fusion.3.sc, s32[4]{0:T(128)} %off.31, bf16[4,512,384]{2,1,0:T(8,128)(2,1)} %get-tuple-element.57.own, bf16[4,512,384]{2,1,0:T(8,128)(2,1)} %copy-done), custom_call_target="tpu_custom_call" | custom-call | bytes 12582912 | tf_op jit(solution)/shard_map/halo/pallas_call | solution.py:138
  84.0 3.8 %collective-permute-start.33 = (bf16[2,896,384]{2,1,0:T(8,128)(2,1)}, bf16[2,896,384]{2,1,0:T(8,128)(2,1)S(1)}, u32[]{:S(2)}, u32[]{:S(2)}) collective-permute-start(bf16[2,896,384]{2,1,0:T(8,128)(2,1)} %get-tuple-element.65), channel_id=1, source_target_pairs={{0,120},{4,124},{8,0},{12,4},{16,8},{20,12},{24,16},{28,20},{32,24... | collective-permute-start | bytes 4128776 | tf_op jit(solution)/shard_map/ppermute | solution.py:567
  87.8 18.9 %attn.2 = (bf16[1024,384]{1,0:T(8,128)(2,1)}, f32[2,1024,384]{2,1,0:T(8,128)}, f32[3,8,1024]{2,1,0:T(8,128)}, bf16[2,512,384]{2,1,0:T(8,128)(2,1)}) custom-call(s32[8]{0:T(128)} %compare_select_fusion.3.sc, s32[4]{0:T(128)} %off.31, bf16[4,512,384]{2,1,0:T(8,128)(2,1)} %get-tuple-element.39.own, bf16[4,512,384]{2,1,0:T(8,128)(2,1)} %copy-done.1, ...), custom_call_target="tpu_custom_call" | custom-call | flops 12079595520 | bytes 12000000 | tf_op jit(solution)/shard_map/attn/pallas_call | solution.py:413
  111.7 10.3 %collective-permute-done.25.halo = bf16[2,896,384]{2,1,0:T(8,128)(2,1)} collective-permute-done((bf16[2,896,384]{2,1,0:T(8,128)(2,1)}, bf16[2,896,384]{2,1,0:T(8,128)(2,1)}, u32[]{:S(2)}, u32[]{:S(2)}) %collective-permute-start.25) | collective-permute-done | bytes 1376288 | tf_op jit(solution)/shard_map/ppermute | solution.py:567
  123.5 18.9 %attn.3 = (bf16[1024,384]{1,0:T(8,128)(2,1)}, f32[2,1024,384]{2,1,0:T(8,128)}, f32[3,8,1024]{2,1,0:T(8,128)}, bf16[2,512,384]{2,1,0:T(8,128)(2,1)}) custom-call(s32[8]{0:T(128)} %compare_select_fusion.3.sc, s32[4]{0:T(128)} %off.31, bf16[4,512,384]{2,1,0:T(8,128)(2,1)} %get-tuple-element.57.own, bf16[4,512,384]{2,1,0:T(8,128)(2,1)} %copy-done, ...), custom_call_target="tpu_custom_call" | custom-call | flops 12079595520 | bytes 12000000 | tf_op jit(solution)/shard_map/attn/pallas_call | solution.py:413
  142.3 14.4 %collective-permute-done.18 = bf16[2,128,384]{2,1,0:T(8,128)(2,1)S(1)} collective-permute-done((bf16[2,128,384]{2,1,0:T(8,128)(2,1)S(1)}, bf16[2,128,384]{2,1,0:T(8,128)(2,1)S(1)}, u32[]{:S(2)}, u32[]{:S(2)}) %collective-permute-start.18) | collective-permute-done | bytes 196640 | tf_op jit(solution)/shard_map/ppermute | solution.py:567
  162.6 3.5 %collective-permute-start.36 = (bf16[2,128,384]{2,1,0:T(8,128)(2,1)S(1)}, bf16[2,128,384]{2,1,0:T(8,128)(2,1)S(1)}, u32[]{:S(2)}, u32[]{:S(2)}) collective-permute-start(bf16[2,128,384]{2,1,0:T(8,128)(2,1)S(1)} %get-tuple-element.77), channel_id=1, source_target_pairs={{0,64},{4,68},{8,72},{12,76},{16,80},{20,84},{24,88},{28,92},{32,9... | collective-permute-start | bytes 589832 | tf_op jit(solution)/shard_map/ppermute | solution.py:567
  166.1 3.9 %collective-permute-done.21.refs_1_ = bf16[2,128,384]{2,1,0:T(8,128)(2,1)S(1)} collective-permute-done((bf16[2,128,384]{2,1,0:T(8,128)(2,1)S(1)}, bf16[2,128,384]{2,1,0:T(8,128)(2,1)S(1)}, u32[]{:S(2)}, u32[]{:S(2)}) %collective-permute-start.21) | collective-permute-done | bytes 196640 | tf_op jit(solution)/shard_map/ppermute | solution.py:567
  172.4 7.9 %later.2.dkv = f32[2,1024,384]{2,1,0:T(8,128)} custom-call(s32[8]{0:T(128)} %compare_select_fusion.3.sc, s32[4]{0:T(128)} %off.31, bf16[4,512,384]{2,1,0:T(8,128)(2,1)} %get-tuple-element.39.own, bf16[4,512,384]{2,1,0:T(8,128)(2,1)} %copy-done.1, bf16[2,896,384]{2,1,0:T(8,128)(2,1)} %copy-done.8, f32[3,8,1024]{2,1,0:T(8,128)} %copy-done.31, ...), custom_call_target="tpu_custom_call" | custom-call | flops 2818572288 | bytes 12000000 | tf_op jit(solution)/shard_map/later/pallas_call | solution.py:382
  181.1 5.3 %finish.2 = (bf16[2,3,128,384]{3,2,1,0:T(8,128)(2,1)}, bf16[2,3,128,384]{3,2,1,0:T(8,128)(2,1)}, bf16[2,3,128,384]{3,2,1,0:T(8,128)(2,1)}, bf16[2,3,128,384]{3,2,1,0:T(8,128)(2,1)}) custom-call(s32[8]{0:T(128)} %compare_select_fusion.3.sc, s32[4]{0:T(128)} %off.31, f32[2,1024,384]{2,1,0:T(8,128)} %later.2.dkv, bf16[2,128,384]{2,1,0:T(8,128)(2,1)} %copy-done.13, ...), custom_call_target="tpu_custom_call" | custom-call | bytes 7864320 | tf_op jit(solution)/shard_map/finish/pallas_call | solution.py:473
  195.6 3.4 %collective-permute-done.34.stat = f32[3,8,1024]{2,1,0:T(8,128)S(1)} collective-permute-done((f32[3,8,1024]{2,1,0:T(8,128)S(1)}, f32[3,8,1024]{2,1,0:T(8,128)S(1)}, u32[]{:S(2)}, u32[]{:S(2)}) %collective-permute-start.34) | collective-permute-done | bytes 98336 | tf_op jit(solution)/shard_map/ppermute | solution.py:567
  203.6 7.8 %later.3.dkv = f32[2,1024,384]{2,1,0:T(8,128)} custom-call(s32[8]{0:T(128)} %compare_select_fusion.3.sc, s32[4]{0:T(128)} %off.31, bf16[4,512,384]{2,1,0:T(8,128)(2,1)} %get-tuple-element.57.own, bf16[4,512,384]{2,1,0:T(8,128)(2,1)} %copy-done, bf16[2,896,384]{2,1,0:T(8,128)(2,1)} %copy-done.7, f32[3,8,1024]{2,1,0:T(8,128)} %copy-done.32, ...), custom_call_target="tpu_custom_call" | custom-call | flops 2818572288 | bytes 12000000 | tf_op jit(solution)/shard_map/later/pallas_call | solution.py:382
  212.7 4.6 %finish.3 = (bf16[2,2,128,384]{3,2,1,0:T(8,128)(2,1)}, bf16[2,2,128,384]{3,2,1,0:T(8,128)(2,1)}, bf16[2,2,128,384]{3,2,1,0:T(8,128)(2,1)}, bf16[2,2,128,384]{3,2,1,0:T(8,128)(2,1)}) custom-call(s32[8]{0:T(128)} %compare_select_fusion.3.sc, s32[4]{0:T(128)} %off.31, f32[2,1024,384]{2,1,0:T(8,128)} %later.3.dkv, bf16[2,128,384]{2,1,0:T(8,128)(2,1)} %copy-done.14, ...), custom_call_target="tpu_custom_call" | custom-call | bytes 7864320 | tf_op jit(solution)/shard_map/finish/pallas_call | solution.py:473
  222.3 8.5 %collective-permute-done.41.refs_6_ = bf16[2,2,128,384]{3,2,1,0:T(8,128)(2,1)S(1)} collective-permute-done((bf16[2,2,128,384]{3,2,1,0:T(8,128)(2,1)}, bf16[2,2,128,384]{3,2,1,0:T(8,128)(2,1)S(1)}, u32[]{:S(2)}, u32[]{:S(2)}) %collective-permute-start.41) | collective-permute-done | bytes 393248 | tf_op jit(solution)/shard_map/ppermute | solution.py:567
  234.8 4.0 %collective-permute-start.13 = (bf16[2,1,128,384]{3,2,1,0:T(8,128)(2,1)}, bf16[2,1,128,384]{3,2,1,0:T(8,128)(2,1)S(1)}, u32[]{:S(2)}, u32[]{:S(2)}) collective-permute-start(bf16[2,1,128,384]{3,2,1,0:T(8,128)(2,1)} %get-tuple-element.51), channel_id=1, source_target_pairs={{0,2},{1,3},{2,0},{3,1},{4,6},{5,7},{6,4},{7,5},{8,10},{9,11},{10,... | collective-permute-start | bytes 589832 | tf_op jit(solution)/shard_map/ppermute | solution.py:567
  239.7 3.8 %collective-permute-done.12.refs_1_ = bf16[2,1,128,384]{3,2,1,0:T(8,128)(2,1)S(1)} collective-permute-done((bf16[2,1,128,384]{3,2,1,0:T(8,128)(2,1)}, bf16[2,1,128,384]{3,2,1,0:T(8,128)(2,1)S(1)}, u32[]{:S(2)}, u32[]{:S(2)}) %collective-permute-start.12) | collective-permute-done | bytes 196640 | tf_op jit(solution)/shard_map/ppermute | solution.py:567
  243.5 5.0 %collective-permute-done.13.refs_2_ = bf16[2,1,128,384]{3,2,1,0:T(8,128)(2,1)S(1)} collective-permute-done((bf16[2,1,128,384]{3,2,1,0:T(8,128)(2,1)}, bf16[2,1,128,384]{3,2,1,0:T(8,128)(2,1)S(1)}, u32[]{:S(2)}, u32[]{:S(2)}) %collective-permute-start.13) | collective-permute-done | bytes 196640 | tf_op jit(solution)/shard_map/ppermute | solution.py:567
  250.6 4.7 %place.3 = (bf16[128,6144]{1,0:T(8,128)(2,1)}, bf16[128,6144]{1,0:T(8,128)(2,1)}) custom-call(s32[8]{0:T(128)} %compare_select_fusion.3.sc, s32[4]{0:T(128)} %off.31, bf16[2,3,128,384]{3,2,1,0:T(8,128)(2,1)} %get-tuple-element.61.refs_5_.refs_0_, bf16[2,3,128,384]{3,2,1,0:T(8,128)(2,1)} %copy-done.4, bf16[2,3,128,384]{3,2,1,0:T(8,128)(2,1)} %copy-done.5, ...), custom_call_target="tpu_custom_call" | custom-call | bytes 6291456 | tf_op jit(solution)/shard_map/place/pallas_call | solution.py:545
  256.1 3.4 %place.2 = bf16[128,6144]{1,0:T(8,128)(2,1)} custom-call(s32[8]{0:T(128)} %compare_select_fusion.3.sc, s32[4]{0:T(128)} %off.31, bf16[2,1,128,384]{3,2,1,0:T(8,128)(2,1)} %get-tuple-element.49.refs_0_, bf16[2,1,128,384]{3,2,1,0:T(8,128)(2,1)} %copy-done.16, bf16[2,1,128,384]{3,2,1,0:T(8,128)(2,1)} %copy-done.17, bf16[2,1,128,384]{3,2,1,0:T(8,128)(2,1)} %copy-done.18, ...), custom_call_target="tpu_custom_call" | custom-call | bytes 3145728 | tf_op jit(solution)/shard_map/place/pallas_call | solution.py:545
  (197 shorter events, 80.4 us)
Async XLA Ops:
  9.2 63.9 %collective-permute-start.24 = (bf16[4,512,384]{2,1,0:T(8,128)(2,1)}, bf16[4,512,384]{2,1,0:T(8,128)(2,1)S(1)}, u32[]{:S(2)}, u32[]{:S(2)}) collective-permute-start(bf16[4,512,384]{2,1,0:T(8,128)(2,1)} %get-tuple-element.58), channel_id=1, source_target_pairs={{0,4},{4,0},{8,12},{12,8},{16,20},{20,16},{24,28},{28,24},{32,36},... | collective-permute-start | bytes 4718600 | tf_op jit(solution)/shard_map/ppermute | solution.py:567
  15.9 68.0 %collective-permute-start.1 = (bf16[2,896,384]{2,1,0:T(8,128)(2,1)}, bf16[2,896,384]{2,1,0:T(8,128)(2,1)S(1)}, u32[]{:S(2)}, u32[]{:S(2)}) collective-permute-start(bf16[2,896,384]{2,1,0:T(8,128)(2,1)} %get-tuple-element.41), channel_id=1, source_target_pairs={{0,8},{4,12},{8,16},{12,20},{16,24},{20,28},{24,32},{28,36},{32,40... | collective-permute-start | bytes 4128776 | tf_op jit(solution)/shard_map/ppermute | solution.py:567
  28.2 26.6 %collective-permute-start.4 = (bf16[2,32,768]{2,1,0:T(8,128)(2,1)}, bf16[2,32,768]{2,1,0:T(8,128)(2,1)S(1)}, u32[]{:S(2)}, u32[]{:S(2)}) collective-permute-start(bf16[2,32,768]{2,1,0:T(8,128)(2,1)} %get-tuple-element.45), channel_id=1, source_target_pairs={{0,16},{4,20},{8,24},{12,28},{16,0},{20,4},{24,8},{28,12},{32,48},... | collective-permute-start | bytes 294920 | tf_op jit(solution)/shard_map/ppermute | solution.py:567
  29.8 24.9 %collective-permute-start.5 = (bf16[2,32,768]{2,1,0:T(8,128)(2,1)}, bf16[2,32,768]{2,1,0:T(8,128)(2,1)S(1)}, u32[]{:S(2)}, u32[]{:S(2)}) collective-permute-start(bf16[2,32,768]{2,1,0:T(8,128)(2,1)} %get-tuple-element.46), channel_id=1, source_target_pairs={{0,8},{4,12},{8,16},{12,20},{16,24},{20,28},{24,0},{28,4},{32,40},... | collective-permute-start | bytes 294920 | tf_op jit(solution)/shard_map/ppermute | solution.py:567
  73.1 34.8 %collective-permute-start.26 = (bf16[2,128,384]{2,1,0:T(8,128)(2,1)S(1)}, bf16[2,128,384]{2,1,0:T(8,128)(2,1)S(1)}, u32[]{:S(2)}, u32[]{:S(2)}) collective-permute-start(bf16[2,128,384]{2,1,0:T(8,128)(2,1)S(1)} %get-tuple-element.81.s0), channel_id=1, source_target_pairs={{0,32},{4,36},{8,40},{12,44},{16,48},{20,52},{24,56},{28,60},{32,6... | collective-permute-start | bytes 589832 | tf_op jit(solution)/shard_map/ppermute | solution.py:567
  80.3 28.8 %collective-permute-start.27 = (bf16[2,128,384]{2,1,0:T(8,128)(2,1)S(1)}, bf16[2,128,384]{2,1,0:T(8,128)(2,1)S(1)}, u32[]{:S(2)}, u32[]{:S(2)}) collective-permute-start(bf16[2,128,384]{2,1,0:T(8,128)(2,1)S(1)} %get-tuple-element.81.s0), channel_id=1, source_target_pairs={{0,64},{4,68},{8,72},{12,76},{16,80},{20,84},{24,88},{28,92},{32,9... | collective-permute-start | bytes 589832 | tf_op jit(solution)/shard_map/ppermute | solution.py:567
  81.5 30.1 %collective-permute-start.28 = (bf16[2,128,384]{2,1,0:T(8,128)(2,1)S(1)}, bf16[2,128,384]{2,1,0:T(8,128)(2,1)S(1)}, u32[]{:S(2)}, u32[]{:S(2)}) collective-permute-start(bf16[2,128,384]{2,1,0:T(8,128)(2,1)S(1)} %get-tuple-element.81.s0), channel_id=1, source_target_pairs={{0,96},{4,100},{8,104},{12,108},{16,112},{20,116},{24,120},{28,124... | collective-permute-start | bytes 589832 | tf_op jit(solution)/shard_map/ppermute | solution.py:567
  83.6 38.4 %collective-permute-start.25 = (bf16[2,896,384]{2,1,0:T(8,128)(2,1)}, bf16[2,896,384]{2,1,0:T(8,128)(2,1)}, u32[]{:S(2)}, u32[]{:S(2)}) collective-permute-start(bf16[2,896,384]{2,1,0:T(8,128)(2,1)} %get-tuple-element.59), channel_id=1, source_target_pairs={{0,8},{4,12},{8,16},{12,20},{16,24},{20,28},{24,32},{28,36},{32,40... | collective-permute-start | bytes 4128776 | tf_op jit(solution)/shard_map/ppermute | solution.py:567
  84.0 109.2 %collective-permute-start.33 = (bf16[2,896,384]{2,1,0:T(8,128)(2,1)}, bf16[2,896,384]{2,1,0:T(8,128)(2,1)S(1)}, u32[]{:S(2)}, u32[]{:S(2)}) collective-permute-start(bf16[2,896,384]{2,1,0:T(8,128)(2,1)} %get-tuple-element.65), channel_id=1, source_target_pairs={{0,120},{4,124},{8,0},{12,4},{16,8},{20,12},{24,16},{28,20},{32,24... | collective-permute-start | bytes 4128776 | tf_op jit(solution)/shard_map/ppermute | solution.py:567
  107.9 54.5 %collective-permute-start.16 = (bf16[2,896,384]{2,1,0:T(8,128)(2,1)S(1)}, bf16[2,896,384]{2,1,0:T(8,128)(2,1)S(1)}, u32[]{:S(2)}, u32[]{:S(2)}) collective-permute-start(bf16[2,896,384]{2,1,0:T(8,128)(2,1)S(1)} %copy-done.36), channel_id=1, source_target_pairs={{0,120},{4,124},{8,0},{12,4},{16,8},{20,12},{24,16},{28,20},{32,24... | collective-permute-start | bytes 4128776 | tf_op jit(solution)/shard_map/ppermute | solution.py:567
  109.0 47.7 %collective-permute-start.18 = (bf16[2,128,384]{2,1,0:T(8,128)(2,1)S(1)}, bf16[2,128,384]{2,1,0:T(8,128)(2,1)S(1)}, u32[]{:S(2)}, u32[]{:S(2)}) collective-permute-start(bf16[2,128,384]{2,1,0:T(8,128)(2,1)S(1)} %get-tuple-element.78), channel_id=1, source_target_pairs={{0,96},{4,100},{8,104},{12,108},{16,112},{20,116},{24,120},{28,124... | collective-permute-start | bytes 589832 | tf_op jit(solution)/shard_map/ppermute | solution.py:567
  111.7 48.3 %collective-permute-start.19 = (bf16[2,128,384]{2,1,0:T(8,128)(2,1)S(1)}, bf16[2,128,384]{2,1,0:T(8,128)(2,1)S(1)}, u32[]{:S(2)}, u32[]{:S(2)}) collective-permute-start(bf16[2,128,384]{2,1,0:T(8,128)(2,1)S(1)} %get-tuple-element.80), channel_id=1, source_target_pairs={{0,64},{4,68},{8,72},{12,76},{16,80},{20,84},{24,88},{28,92},{32,9... | collective-permute-start | bytes 589832 | tf_op jit(solution)/shard_map/ppermute | solution.py:567
  121.9 38.0 %collective-permute-start.20 = (bf16[2,128,384]{2,1,0:T(8,128)(2,1)S(1)}, bf16[2,128,384]{2,1,0:T(8,128)(2,1)S(1)}, u32[]{:S(2)}, u32[]{:S(2)}) collective-permute-start(bf16[2,128,384]{2,1,0:T(8,128)(2,1)S(1)} %get-tuple-element.79), channel_id=1, source_target_pairs={{0,32},{4,36},{8,40},{12,44},{16,48},{20,52},{24,56},{28,60},{32,6... | collective-permute-start | bytes 589832 | tf_op jit(solution)/shard_map/ppermute | solution.py:567
  162.4 25.5 %collective-permute-start.35 = (bf16[2,128,384]{2,1,0:T(8,128)(2,1)S(1)}, bf16[2,128,384]{2,1,0:T(8,128)(2,1)S(1)}, u32[]{:S(2)}, u32[]{:S(2)}) collective-permute-start(bf16[2,128,384]{2,1,0:T(8,128)(2,1)S(1)} %get-tuple-element.75), channel_id=1, source_target_pairs={{0,96},{4,100},{8,104},{12,108},{16,112},{20,116},{24,120},{28,124... | collective-permute-start | bytes 589832 | tf_op jit(solution)/shard_map/ppermute | solution.py:567
  162.6 28.0 %collective-permute-start.36 = (bf16[2,128,384]{2,1,0:T(8,128)(2,1)S(1)}, bf16[2,128,384]{2,1,0:T(8,128)(2,1)S(1)}, u32[]{:S(2)}, u32[]{:S(2)}) collective-permute-start(bf16[2,128,384]{2,1,0:T(8,128)(2,1)S(1)} %get-tuple-element.77), channel_id=1, source_target_pairs={{0,64},{4,68},{8,72},{12,76},{16,80},{20,84},{24,88},{28,92},{32,9... | collective-permute-start | bytes 589832 | tf_op jit(solution)/shard_map/ppermute | solution.py:567
  170.0 22.0 %collective-permute-start.37 = (bf16[2,128,384]{2,1,0:T(8,128)(2,1)S(1)}, bf16[2,128,384]{2,1,0:T(8,128)(2,1)S(1)}, u32[]{:S(2)}, u32[]{:S(2)}) collective-permute-start(bf16[2,128,384]{2,1,0:T(8,128)(2,1)S(1)} %get-tuple-element.76), channel_id=1, source_target_pairs={{0,32},{4,36},{8,40},{12,44},{16,48},{20,52},{24,56},{28,60},{32,6... | collective-permute-start | bytes 589832 | tf_op jit(solution)/shard_map/ppermute | solution.py:567
  186.4 32.7 %collective-permute-start.29 = (bf16[2,3,128,384]{3,2,1,0:T(8,128)(2,1)}, bf16[2,3,128,384]{3,2,1,0:T(8,128)(2,1)S(1)}, u32[]{:S(2)}, u32[]{:S(2)}) collective-permute-start(bf16[2,3,128,384]{3,2,1,0:T(8,128)(2,1)} %get-tuple-element.62), channel_id=1, source_target_pairs={{0,1},{1,2},{2,3},{3,0},{4,5},{5,6},{6,7},{7,4},{8,9},{9,10},{10,1... | collective-permute-start | bytes 1769480 | tf_op jit(solution)/shard_map/ppermute | solution.py:567
  187.9 33.0 %collective-permute-start.30 = (bf16[2,3,128,384]{3,2,1,0:T(8,128)(2,1)}, bf16[2,3,128,384]{3,2,1,0:T(8,128)(2,1)S(1)}, u32[]{:S(2)}, u32[]{:S(2)}) collective-permute-start(bf16[2,3,128,384]{3,2,1,0:T(8,128)(2,1)} %get-tuple-element.63), channel_id=1, source_target_pairs={{0,2},{1,3},{2,0},{3,1},{4,6},{5,7},{6,4},{7,5},{8,10},{9,11},{10,... | collective-permute-start | bytes 1769480 | tf_op jit(solution)/shard_map/ppermute | solution.py:567
  190.6 30.3 %collective-permute-start.31 = (bf16[2,3,128,384]{3,2,1,0:T(8,128)(2,1)}, bf16[2,3,128,384]{3,2,1,0:T(8,128)(2,1)S(1)}, u32[]{:S(2)}, u32[]{:S(2)}) collective-permute-start(bf16[2,3,128,384]{3,2,1,0:T(8,128)(2,1)} %get-tuple-element.64), channel_id=1, source_target_pairs={{0,3},{1,0},{2,1},{3,2},{4,7},{5,4},{6,5},{7,6},{8,11},{9,8},{10,9... | collective-permute-start | bytes 1769480 | tf_op jit(solution)/shard_map/ppermute | solution.py:567
  217.4 13.4 %collective-permute-start.41 = (bf16[2,2,128,384]{3,2,1,0:T(8,128)(2,1)}, bf16[2,2,128,384]{3,2,1,0:T(8,128)(2,1)S(1)}, u32[]{:S(2)}, u32[]{:S(2)}) collective-permute-start(bf16[2,2,128,384]{3,2,1,0:T(8,128)(2,1)} %get-tuple-element.70), channel_id=1, source_target_pairs={{0,1},{1,2},{2,3},{3,0},{4,5},{5,6},{6,7},{7,4},{8,9},{9,10},{10,1... | collective-permute-start | bytes 1179656 | tf_op jit(solution)/shard_map/ppermute | solution.py:567
  218.0 12.8 %collective-permute-start.42 = (bf16[2,2,128,384]{3,2,1,0:T(8,128)(2,1)}, bf16[2,2,128,384]{3,2,1,0:T(8,128)(2,1)S(1)}, u32[]{:S(2)}, u32[]{:S(2)}) collective-permute-start(bf16[2,2,128,384]{3,2,1,0:T(8,128)(2,1)} %get-tuple-element.71), channel_id=1, source_target_pairs={{0,2},{1,3},{2,0},{3,1},{4,6},{5,7},{6,4},{7,5},{8,10},{9,11},{10,... | collective-permute-start | bytes 1179656 | tf_op jit(solution)/shard_map/ppermute | solution.py:567
  221.7 27.0 %collective-permute-start.32 = (bf16[4,3,128,384]{3,2,1,0:T(8,128)(2,1)S(1)}, bf16[4,3,128,384]{3,2,1,0:T(8,128)(2,1)S(1)}, u32[]{:S(2)}, u32[]{:S(2)}) collective-permute-start(bf16[4,3,128,384]{3,2,1,0:T(8,128)(2,1)S(1)} %pad_maximum_fusion), channel_id=1, source_target_pairs={{0,4},{4,0},{8,12},{12,8},{16,20},{20,16},{24,28},{28,24},{32,36},... | collective-permute-start | bytes 3538952 | tf_op jit(solution)/shard_map/ppermute | solution.py:567
  231.9 16.8 %collective-permute-start.44 = (bf16[4,2,128,384]{3,2,1,0:T(8,128)(2,1)S(1)}, bf16[4,2,128,384]{3,2,1,0:T(8,128)(2,1)S(1)}, u32[]{:S(2)}, u32[]{:S(2)}) collective-permute-start(bf16[4,2,128,384]{3,2,1,0:T(8,128)(2,1)S(1)} %pad_maximum_fusion.1), channel_id=1, source_target_pairs={{0,4},{4,0},{8,12},{12,8},{16,20},{20,16},{24,28},{28,24},{32,36},... | collective-permute-start | bytes 2359304 | tf_op jit(solution)/shard_map/ppermute | solution.py:567
  234.8 13.7 %collective-permute-start.13 = (bf16[2,1,128,384]{3,2,1,0:T(8,128)(2,1)}, bf16[2,1,128,384]{3,2,1,0:T(8,128)(2,1)S(1)}, u32[]{:S(2)}, u32[]{:S(2)}) collective-permute-start(bf16[2,1,128,384]{3,2,1,0:T(8,128)(2,1)} %get-tuple-element.51), channel_id=1, source_target_pairs={{0,2},{1,3},{2,0},{3,1},{4,6},{5,7},{6,4},{7,5},{8,10},{9,11},{10,... | collective-permute-start | bytes 589832 | tf_op jit(solution)/shard_map/ppermute | solution.py:567
  (67 other events, 563.9 us)
